TPU v7x, 128 devices: a whole 4x4x4 slice. The times are simulated.
128 devices in a mesh: tm: 2 (over core), cell: 64 (over z, y, x).
Axes of the slice: x: 4, y: 4, z: 4, core: 2. Of those that a mesh axis runs over, the one named last changes fastest.
Arguments:
- block_rows: int32 [2, 4096], P('tm', 'cell'), may hold values from 0 to 255, as said below
- block_cols: int32 [2, 4096], P('tm', 'cell'), may hold values from 0 to 255, as said below
- block_values: bfloat16 [2, 4096, 128, 128], P('tm', 'cell'), as said below
- growth: float32 [2, 32768], P('tm', 'cell'), may hold values from 0.5 to 4
- first_labels: int32 [8, 32768], P(None, 'cell'), may hold values from 0 to 15, as said below
- last_labels: int32 [8, 32768], P(None, 'cell'), may hold values from 0 to 15
Outputs:
- forward_mass: bfloat16 [2, 128, 32768], P('tm', None, 'cell')
- fate: bfloat16 [2, 128, 32768], P('tm', None, 'cell')
Inputs may be any that keep to these rules, and one draw needn't show every extreme that they name: `block_rows`: the slots n of a coupling with n // 64 = c name row blocks c * 4 to (c + 1) * 4 - 1 only, and each row block is named by exactly 16 slots of each coupling. `block_cols`: A slot's column block differs from its row block by at most 4; a pair of row and column block may stand in several slots, whose blocks then add. `block_values`: every entry is positive. `first_labels`: in every panel each of the 16 types labels exactly 2048 cells.
All inputs are finite; a program needn't handle non-finite values.
Results may differ from a plain program's by a relative error of at most 0.006.
Values may be sent and summed in bfloat16 or wider, within the bound.
A program may use at most 64 MiB of HBM per device.

v0:
```python
import jax
import jax.numpy as jnp
from jax import lax
from jax.sharding import PartitionSpec as P

CELL_TYPES = 16
BAND_REACH = 4


def extended(array, sides, width):
    for axis, dim in sides:
        devices, length = (lax.axis_size(axis), array.shape[dim])
        up = [(i, (i + 1) % devices) for i in range(devices - 1)]
        down = [(j, i) for i, j in up]
        last = lax.slice_in_dim(array, length - width, length, axis=dim)
        initial = lax.slice_in_dim(array, 0, width, axis=dim)
        before = lax.ppermute(last, axis, up)
        after = lax.ppermute(initial, axis, down)
        array = jnp.concatenate([before, array, after], axis=dim)
    return array


def shifted(block, axis, distance):
    devices = range(lax.axis_size(axis))
    route = [(i - distance, i) for i in devices if i - distance in devices]
    return lax.ppermute(block, axis, route)


def seed_stack(labels, front_index, width):
    picked = lax.dynamic_slice_in_dim(labels, front_index * width, width, 0)
    marks = picked[:, None, :] == jnp.arange(CELL_TYPES, dtype=jnp.int32)[None, :, None]
    return marks.astype(jnp.bfloat16).reshape(width * CELL_TYPES, labels.shape[1])


def on_device(block_rows, block_cols, block_values, growth, first_labels, last_labels):
    chain_len = lax.axis_size("tm")
    tm_index = lax.axis_index("tm")
    cell_index = lax.axis_index("cell")
    cell_count = lax.axis_size("cell")
    growth_row = growth[0]
    block_side = block_values.shape[2]
    dev_cells = growth_row.shape[0]
    dev_blocks = dev_cells // block_side
    slot_count = block_rows.shape[1]
    per_row = slot_count // dev_blocks
    window = dev_blocks + 2 * BAND_REACH
    all_cells = dev_cells * cell_count
    panels = first_labels.shape[0]
    local_rows = block_rows[0] - cell_index * dev_blocks
    order = jnp.argsort(local_rows, stable=True)
    blocks = jnp.take(block_values[0], order, axis=0)
    offsets = jnp.take(block_cols[0] - block_rows[0], order, axis=0).reshape(dev_blocks, per_row)

    def forward_step(stack_in):
        height = stack_in.shape[0]
        scaled = (stack_in.astype(jnp.float32) / growth_row[None, :]).astype(jnp.bfloat16)
        by_block = jnp.swapaxes(scaled.reshape(height, dev_blocks, block_side), 0, 1)
        picked = jnp.repeat(by_block, per_row, axis=0)
        carried = jnp.einsum("sqk,skl->sql", picked, blocks, preferred_element_type=jnp.float32)
        grouped = carried.reshape(dev_blocks, per_row, height, block_side)
        spread = jnp.zeros((window, height, block_side), jnp.float32)
        for shift_by in range(-BAND_REACH, BAND_REACH + 1):
            hit = (offsets == shift_by)[:, :, None, None]
            partial_sum = jnp.sum(jnp.where(hit, grouped, 0.0), axis=1)
            low = BAND_REACH + shift_by
            spread = spread + jnp.pad(
                partial_sum, ((low, window - dev_blocks - low), (0, 0), (0, 0))
            )
        spread = jnp.transpose(spread, (1, 0, 2))
        inside = spread[:, BAND_REACH : BAND_REACH + dev_blocks]
        outside = jnp.concatenate(
            [spread[:, :BAND_REACH], spread[:, BAND_REACH + dev_blocks :]], axis=1
        )
        margin = extended(outside.astype(jnp.bfloat16), (("cell", 1),), BAND_REACH).astype(
            outside.dtype
        )
        inside = inside.at[:, :BAND_REACH].add(margin[:, :BAND_REACH])
        inside = inside.at[:, dev_blocks - BAND_REACH :].add(margin[:, 3 * BAND_REACH :])
        totals = lax.psum(jnp.sum(inside, axis=(1, 2)), "cell")
        scaled_mass = inside * (all_cells / totals)[:, None, None]
        return scaled_mass.astype(jnp.bfloat16).reshape(height, dev_cells)

    def backward_step(stack_in):
        height = stack_in.shape[0]
        shaped = stack_in.reshape(height, dev_blocks, block_side)
        widened = extended(shaped, (("cell", 1),), BAND_REACH)
        widened = jnp.swapaxes(widened, 0, 1)
        picked = jnp.zeros((dev_blocks, per_row, height, block_side), jnp.bfloat16)
        for shift_by in range(-BAND_REACH, BAND_REACH + 1):
            low = BAND_REACH + shift_by
            candidate = widened[low : low + dev_blocks][:, None]
            hit = (offsets == shift_by)[:, :, None, None]
            picked = jnp.where(hit, candidate, picked)
        picked = picked.reshape(slot_count, height, block_side)
        pulled = jnp.einsum("skl,sql->sqk", blocks, picked, preferred_element_type=jnp.float32)
        summed = jnp.sum(pulled.reshape(dev_blocks, per_row, height, block_side), axis=1)
        summed = jnp.transpose(summed, (1, 0, 2))
        grouped = summed.reshape(height // CELL_TYPES, CELL_TYPES, dev_blocks, block_side)
        fates = grouped * (CELL_TYPES / jnp.sum(grouped, axis=1, keepdims=True))
        return fates.astype(jnp.bfloat16).reshape(height, dev_cells)

    def forward_section(step_index, received, stored, width):
        fronts = panels // width
        front_index = step_index - tm_index
        active = (front_index >= 0) & (front_index < fronts)
        bounded = jnp.clip(front_index, 0, fronts - 1)
        seeded = seed_stack(first_labels, bounded, width)
        stack_in = jnp.where((tm_index == 0) | jnp.logical_not(active), seeded, received)
        computed = forward_step(stack_in)
        result = jnp.where(active, computed, jnp.zeros_like(computed))
        updated = lax.dynamic_update_slice_in_dim(stored, result, bounded * width * CELL_TYPES, 0)
        stored = jnp.where(active, updated, stored)
        return (shifted(result, "tm", 1), stored)

    def backward_section(step_index, received, stored, width):
        fronts = panels // width
        front_index = step_index - (chain_len - 1 - tm_index)
        active = (front_index >= 0) & (front_index < fronts)
        bounded = jnp.clip(front_index, 0, fronts - 1)
        seeded = seed_stack(last_labels, bounded, width)
        stack_in = jnp.where(
            (tm_index == chain_len - 1) | jnp.logical_not(active), seeded, received
        )
        computed = backward_step(stack_in)
        result = jnp.where(active, computed, jnp.zeros_like(computed))
        updated = lax.dynamic_update_slice_in_dim(stored, result, bounded * width * CELL_TYPES, 0)
        stored = jnp.where(active, updated, stored)
        return (shifted(result, "tm", -1), stored)

    width = 1
    sections = chain_len + panels // width - 1
    empty_stack = jnp.zeros((width * CELL_TYPES, dev_cells), jnp.bfloat16)
    empty_store = jnp.zeros((panels * CELL_TYPES, dev_cells), jnp.bfloat16)

    def forward_turn(step_index, state_pair):
        return forward_section(step_index, state_pair[0], state_pair[1], width)

    def backward_turn(step_index, state_pair):
        return backward_section(step_index, state_pair[0], state_pair[1], width)

    forward_state = lax.fori_loop(0, sections, forward_turn, (empty_stack, empty_store))
    backward_state = lax.fori_loop(0, sections, backward_turn, (empty_stack, empty_store))
    forward_mass = forward_state[1]
    fate = backward_state[1]
    return (forward_mass[None], fate[None])


def solution(mesh):
    placed = (
        P("tm", "cell"),
        P("tm", "cell"),
        P("tm", "cell", None, None),
        P("tm", "cell"),
        P(None, "cell"),
        P(None, "cell"),
    )
    return jax.shard_map(
        on_device,
        mesh=mesh,
        in_specs=placed,
        out_specs=(P("tm", None, "cell"), P("tm", None, "cell")),
        check_vma=False,
    )
```

profile of v0, /device:TPU:1, one launch (start us, length us, event | category | flops | bytes accessed | tf_op | source)
XLA Modules:
  0.0 1844.1 jit_solution(18438380487693806452)
XLA Ops:
  6.6 3.2 broadcast_select_fusion
  9.8 1688.4 %while.52 = (s32[]{:T(128)}, bf16[16,512]{1,0:T(8,128)(2,1)S(1)}, bf16[128,512]{1,0:T(8,128)(2,1)S(1)}, s32[]{:T(128)}, s32[4,16]{1,0:T(4,128)S(1)}, /*index=5*/...) while((s32[]{:T(128)}, bf16[16,512]{1,0:T(8,128)(2,1)S(1)}, ...), condition=%wide.region_13.14_spmd, body=%wide.region_1.13_spmd.sunk | while | flops 36258392 | bytes 3993719 | solution.py:141
  14.2 4.6 collective-permute-start.1
  19.7 153.6 %psum.15 = f32[16]{0:T(128)S(1)} all-reduce(f32[16]{0:T(128)S(1)} %get-tuple-element.696), channel_id=1, replica_groups=mesh['tm'=2,'cell'=64] {'cell'}, use_global_device_ids=true, to_apply=%region_12.12 | all-reduce | flops 16 | bytes 128 | tf_op jit(solution)/shard_map/while/body/eval_jaxpr/psum | solution.py:79
  174.8 30.6 %collective-permute-done.2 = bf16[16,512]{1,0:T(8,128)(2,1)S(1)} collective-permute-done((bf16[16,512]{1,0:T(8,128)(2,1)S(1)}, bf16[16,512]{1,0:T(8,128)(2,1)S(1)}, u32[]{:S(2)}, u32[]{:S(2)}) %collective-permute-start.2) | collective-permute-done | bytes 16416 | tf_op jit(solution)/shard_map/while/body/eval_jaxpr/ppermute | solution.py:26
  209.6 4.0 collective-permute-start.1
  214.6 146.3 %psum.15 = f32[16]{0:T(128)S(1)} all-reduce(f32[16]{0:T(128)S(1)} %get-tuple-element.696), channel_id=1, replica_groups=mesh['tm'=2,'cell'=64] {'cell'}, use_global_device_ids=true, to_apply=%region_12.12 | all-reduce | flops 16 | bytes 128 | tf_op jit(solution)/shard_map/while/body/eval_jaxpr/psum | solution.py:79
  362.4 29.5 %collective-permute-done.2 = bf16[16,512]{1,0:T(8,128)(2,1)S(1)} collective-permute-done((bf16[16,512]{1,0:T(8,128)(2,1)S(1)}, bf16[16,512]{1,0:T(8,128)(2,1)S(1)}, u32[]{:S(2)}, u32[]{:S(2)}) %collective-permute-start.2) | collective-permute-done | bytes 16416 | tf_op jit(solution)/shard_map/while/body/eval_jaxpr/ppermute | solution.py:26
  396.3 4.0 collective-permute-start.1
  401.2 146.3 %psum.15 = f32[16]{0:T(128)S(1)} all-reduce(f32[16]{0:T(128)S(1)} %get-tuple-element.696), channel_id=1, replica_groups=mesh['tm'=2,'cell'=64] {'cell'}, use_global_device_ids=true, to_apply=%region_12.12 | all-reduce | flops 16 | bytes 128 | tf_op jit(solution)/shard_map/while/body/eval_jaxpr/psum | solution.py:79
  549.0 29.5 %collective-permute-done.2 = bf16[16,512]{1,0:T(8,128)(2,1)S(1)} collective-permute-done((bf16[16,512]{1,0:T(8,128)(2,1)S(1)}, bf16[16,512]{1,0:T(8,128)(2,1)S(1)}, u32[]{:S(2)}, u32[]{:S(2)}) %collective-permute-start.2) | collective-permute-done | bytes 16416 | tf_op jit(solution)/shard_map/while/body/eval_jaxpr/ppermute | solution.py:26
  582.9 4.0 collective-permute-start.1
  587.8 146.3 %psum.15 = f32[16]{0:T(128)S(1)} all-reduce(f32[16]{0:T(128)S(1)} %get-tuple-element.696), channel_id=1, replica_groups=mesh['tm'=2,'cell'=64] {'cell'}, use_global_device_ids=true, to_apply=%region_12.12 | all-reduce | flops 16 | bytes 128 | tf_op jit(solution)/shard_map/while/body/eval_jaxpr/psum | solution.py:79
  735.6 29.5 %collective-permute-done.2 = bf16[16,512]{1,0:T(8,128)(2,1)S(1)} collective-permute-done((bf16[16,512]{1,0:T(8,128)(2,1)S(1)}, bf16[16,512]{1,0:T(8,128)(2,1)S(1)}, u32[]{:S(2)}, u32[]{:S(2)}) %collective-permute-start.2) | collective-permute-done | bytes 16416 | tf_op jit(solution)/shard_map/while/body/eval_jaxpr/ppermute | solution.py:26
  769.5 4.0 collective-permute-start.1
  774.5 146.3 %psum.15 = f32[16]{0:T(128)S(1)} all-reduce(f32[16]{0:T(128)S(1)} %get-tuple-element.696), channel_id=1, replica_groups=mesh['tm'=2,'cell'=64] {'cell'}, use_global_device_ids=true, to_apply=%region_12.12 | all-reduce | flops 16 | bytes 128 | tf_op jit(solution)/shard_map/while/body/eval_jaxpr/psum | solution.py:79
  922.2 29.5 %collective-permute-done.2 = bf16[16,512]{1,0:T(8,128)(2,1)S(1)} collective-permute-done((bf16[16,512]{1,0:T(8,128)(2,1)S(1)}, bf16[16,512]{1,0:T(8,128)(2,1)S(1)}, u32[]{:S(2)}, u32[]{:S(2)}) %collective-permute-start.2) | collective-permute-done | bytes 16416 | tf_op jit(solution)/shard_map/while/body/eval_jaxpr/ppermute | solution.py:26
  956.1 4.0 collective-permute-start.1
  961.1 146.3 %psum.15 = f32[16]{0:T(128)S(1)} all-reduce(f32[16]{0:T(128)S(1)} %get-tuple-element.696), channel_id=1, replica_groups=mesh['tm'=2,'cell'=64] {'cell'}, use_global_device_ids=true, to_apply=%region_12.12 | all-reduce | flops 16 | bytes 128 | tf_op jit(solution)/shard_map/while/body/eval_jaxpr/psum | solution.py:79
  1108.9 29.5 %collective-permute-done.2 = bf16[16,512]{1,0:T(8,128)(2,1)S(1)} collective-permute-done((bf16[16,512]{1,0:T(8,128)(2,1)S(1)}, bf16[16,512]{1,0:T(8,128)(2,1)S(1)}, u32[]{:S(2)}, u32[]{:S(2)}) %collective-permute-start.2) | collective-permute-done | bytes 16416 | tf_op jit(solution)/shard_map/while/body/eval_jaxpr/ppermute | solution.py:26
  1142.7 4.0 collective-permute-start.1
  1147.7 146.3 %psum.15 = f32[16]{0:T(128)S(1)} all-reduce(f32[16]{0:T(128)S(1)} %get-tuple-element.696), channel_id=1, replica_groups=mesh['tm'=2,'cell'=64] {'cell'}, use_global_device_ids=true, to_apply=%region_12.12 | all-reduce | flops 16 | bytes 128 | tf_op jit(solution)/shard_map/while/body/eval_jaxpr/psum | solution.py:79
  1295.5 29.5 %collective-permute-done.2 = bf16[16,512]{1,0:T(8,128)(2,1)S(1)} collective-permute-done((bf16[16,512]{1,0:T(8,128)(2,1)S(1)}, bf16[16,512]{1,0:T(8,128)(2,1)S(1)}, u32[]{:S(2)}, u32[]{:S(2)}) %collective-permute-start.2) | collective-permute-done | bytes 16416 | tf_op jit(solution)/shard_map/while/body/eval_jaxpr/ppermute | solution.py:26
  1329.3 4.0 collective-permute-start.1
  1334.3 146.3 %psum.15 = f32[16]{0:T(128)S(1)} all-reduce(f32[16]{0:T(128)S(1)} %get-tuple-element.696), channel_id=1, replica_groups=mesh['tm'=2,'cell'=64] {'cell'}, use_global_device_ids=true, to_apply=%region_12.12 | all-reduce | flops 16 | bytes 128 | tf_op jit(solution)/shard_map/while/body/eval_jaxpr/psum | solution.py:79
  1482.1 29.5 %collective-permute-done.2 = bf16[16,512]{1,0:T(8,128)(2,1)S(1)} collective-permute-done((bf16[16,512]{1,0:T(8,128)(2,1)S(1)}, bf16[16,512]{1,0:T(8,128)(2,1)S(1)}, u32[]{:S(2)}, u32[]{:S(2)}) %collective-permute-start.2) | collective-permute-done | bytes 16416 | tf_op jit(solution)/shard_map/while/body/eval_jaxpr/ppermute | solution.py:26
  1516.0 4.0 collective-permute-start.1
  1520.9 146.3 %psum.15 = f32[16]{0:T(128)S(1)} all-reduce(f32[16]{0:T(128)S(1)} %get-tuple-element.696), channel_id=1, replica_groups=mesh['tm'=2,'cell'=64] {'cell'}, use_global_device_ids=true, to_apply=%region_12.12 | all-reduce | flops 16 | bytes 128 | tf_op jit(solution)/shard_map/while/body/eval_jaxpr/psum | solution.py:79
  1668.7 29.5 %collective-permute-done.2 = bf16[16,512]{1,0:T(8,128)(2,1)S(1)} collective-permute-done((bf16[16,512]{1,0:T(8,128)(2,1)S(1)}, bf16[16,512]{1,0:T(8,128)(2,1)S(1)}, u32[]{:S(2)}, u32[]{:S(2)}) %collective-permute-start.2) | collective-permute-done | bytes 16416 | tf_op jit(solution)/shard_map/while/body/eval_jaxpr/ppermute | solution.py:26
  1698.9 144.5 %while.53 = (s32[]{:T(128)}, bf16[16,512]{1,0:T(8,128)(2,1)S(1)}, bf16[128,512]{1,0:T(8,128)(2,1)S(1)}, s32[]{:T(128)}, s32[4,16]{1,0:T(4,128)S(1)}, /*index=5*/...) while((s32[]{:T(128)}, bf16[16,512]{1,0:T(8,128)(2,1)S(1)}, ...), condition=%wide.region_17.18_spmd, body=%wide.region_14.17_spmd.sunk | while | flops 35095112 | bytes 3920239 | solution.py:142
  1701.0 4.0 collective-permute-start.4
  1709.9 3.2 collective-permute-start.5
  1716.0 4.5 collective-permute-start.4
  1725.5 3.1 collective-permute-start.5
  1731.5 4.5 collective-permute-start.4
  1741.0 3.1 collective-permute-start.5
  1747.0 4.5 collective-permute-start.4
  1756.5 3.1 collective-permute-start.5
  1762.4 4.5 collective-permute-start.4
  1771.9 3.1 collective-permute-start.5
  1777.9 4.5 collective-permute-start.4
  1787.4 3.1 collective-permute-start.5
  1793.4 5.9 collective-permute-start.4
  1804.3 3.1 collective-permute-start.5
  1810.3 6.7 collective-permute-start.4
  1821.9 3.1 collective-permute-start.5
  1827.9 6.7 collective-permute-start.4
  1839.5 3.1 collective-permute-start.5
  (480 shorter events, 136.2 us)
Async XLA Ops:
  12.9 5.9 collective-permute-start
  14.2 5.4 collective-permute-start.1
  173.4 31.9 %collective-permute-start.2 = (bf16[16,512]{1,0:T(8,128)(2,1)S(1)}, bf16[16,512]{1,0:T(8,128)(2,1)S(1)}, u32[]{:S(2)}, u32[]{:S(2)}) collective-permute-start(bf16[16,512]{1,0:T(8,128)(2,1)S(1)} %copy_bitcast_fusion.4), channel_id=1, source_target_pairs={{0,64},{1,65},{2,66},{3,67},{4,68},{5,69},{6,70},{7,71},{8,72},{9,... | collective-permute-start | bytes 49160 | tf_op jit(solution)/shard_map/while/body/eval_jaxpr/ppermute | solution.py:26
  208.3 5.3 collective-permute-start
  209.6 4.8 collective-permute-start.1
  361.0 30.9 %collective-permute-start.2 = (bf16[16,512]{1,0:T(8,128)(2,1)S(1)}, bf16[16,512]{1,0:T(8,128)(2,1)S(1)}, u32[]{:S(2)}, u32[]{:S(2)}) collective-permute-start(bf16[16,512]{1,0:T(8,128)(2,1)S(1)} %copy_bitcast_fusion.4), channel_id=1, source_target_pairs={{0,64},{1,65},{2,66},{3,67},{4,68},{5,69},{6,70},{7,71},{8,72},{9,... | collective-permute-start | bytes 49160 | tf_op jit(solution)/shard_map/while/body/eval_jaxpr/ppermute | solution.py:26
  395.0 5.3 collective-permute-start
  396.3 4.8 collective-permute-start.1
  547.6 30.9 %collective-permute-start.2 = (bf16[16,512]{1,0:T(8,128)(2,1)S(1)}, bf16[16,512]{1,0:T(8,128)(2,1)S(1)}, u32[]{:S(2)}, u32[]{:S(2)}) collective-permute-start(bf16[16,512]{1,0:T(8,128)(2,1)S(1)} %copy_bitcast_fusion.4), channel_id=1, source_target_pairs={{0,64},{1,65},{2,66},{3,67},{4,68},{5,69},{6,70},{7,71},{8,72},{9,... | collective-permute-start | bytes 49160 | tf_op jit(solution)/shard_map/while/body/eval_jaxpr/ppermute | solution.py:26
  581.6 5.3 collective-permute-start
  582.9 4.8 collective-permute-start.1
  734.2 30.9 %collective-permute-start.2 = (bf16[16,512]{1,0:T(8,128)(2,1)S(1)}, bf16[16,512]{1,0:T(8,128)(2,1)S(1)}, u32[]{:S(2)}, u32[]{:S(2)}) collective-permute-start(bf16[16,512]{1,0:T(8,128)(2,1)S(1)} %copy_bitcast_fusion.4), channel_id=1, source_target_pairs={{0,64},{1,65},{2,66},{3,67},{4,68},{5,69},{6,70},{7,71},{8,72},{9,... | collective-permute-start | bytes 49160 | tf_op jit(solution)/shard_map/while/body/eval_jaxpr/ppermute | solution.py:26
  768.2 5.3 collective-permute-start
  769.5 4.8 collective-permute-start.1
  920.9 30.9 %collective-permute-start.2 = (bf16[16,512]{1,0:T(8,128)(2,1)S(1)}, bf16[16,512]{1,0:T(8,128)(2,1)S(1)}, u32[]{:S(2)}, u32[]{:S(2)}) collective-permute-start(bf16[16,512]{1,0:T(8,128)(2,1)S(1)} %copy_bitcast_fusion.4), channel_id=1, source_target_pairs={{0,64},{1,65},{2,66},{3,67},{4,68},{5,69},{6,70},{7,71},{8,72},{9,... | collective-permute-start | bytes 49160 | tf_op jit(solution)/shard_map/while/body/eval_jaxpr/ppermute | solution.py:26
  954.8 5.3 collective-permute-start
  956.1 4.8 collective-permute-start.1
  1107.5 30.9 %collective-permute-start.2 = (bf16[16,512]{1,0:T(8,128)(2,1)S(1)}, bf16[16,512]{1,0:T(8,128)(2,1)S(1)}, u32[]{:S(2)}, u32[]{:S(2)}) collective-permute-start(bf16[16,512]{1,0:T(8,128)(2,1)S(1)} %copy_bitcast_fusion.4), channel_id=1, source_target_pairs={{0,64},{1,65},{2,66},{3,67},{4,68},{5,69},{6,70},{7,71},{8,72},{9,... | collective-permute-start | bytes 49160 | tf_op jit(solution)/shard_map/while/body/eval_jaxpr/ppermute | solution.py:26
  1141.4 5.3 collective-permute-start
  1142.7 4.8 collective-permute-start.1
  1294.1 30.9 %collective-permute-start.2 = (bf16[16,512]{1,0:T(8,128)(2,1)S(1)}, bf16[16,512]{1,0:T(8,128)(2,1)S(1)}, u32[]{:S(2)}, u32[]{:S(2)}) collective-permute-start(bf16[16,512]{1,0:T(8,128)(2,1)S(1)} %copy_bitcast_fusion.4), channel_id=1, source_target_pairs={{0,64},{1,65},{2,66},{3,67},{4,68},{5,69},{6,70},{7,71},{8,72},{9,... | collective-permute-start | bytes 49160 | tf_op jit(solution)/shard_map/while/body/eval_jaxpr/ppermute | solution.py:26
  1328.0 5.3 collective-permute-start
  1329.3 4.8 collective-permute-start.1
  1480.7 30.9 %collective-permute-start.2 = (bf16[16,512]{1,0:T(8,128)(2,1)S(1)}, bf16[16,512]{1,0:T(8,128)(2,1)S(1)}, u32[]{:S(2)}, u32[]{:S(2)}) collective-permute-start(bf16[16,512]{1,0:T(8,128)(2,1)S(1)} %copy_bitcast_fusion.4), channel_id=1, source_target_pairs={{0,64},{1,65},{2,66},{3,67},{4,68},{5,69},{6,70},{7,71},{8,72},{9,... | collective-permute-start | bytes 49160 | tf_op jit(solution)/shard_map/while/body/eval_jaxpr/ppermute | solution.py:26
  1514.7 5.3 collective-permute-start
  1516.0 4.8 collective-permute-start.1
  1667.3 30.9 %collective-permute-start.2 = (bf16[16,512]{1,0:T(8,128)(2,1)S(1)}, bf16[16,512]{1,0:T(8,128)(2,1)S(1)}, u32[]{:S(2)}, u32[]{:S(2)}) collective-permute-start(bf16[16,512]{1,0:T(8,128)(2,1)S(1)} %copy_bitcast_fusion.4), channel_id=1, source_target_pairs={{0,64},{1,65},{2,66},{3,67},{4,68},{5,69},{6,70},{7,71},{8,72},{9,... | collective-permute-start | bytes 49160 | tf_op jit(solution)/shard_map/while/body/eval_jaxpr/ppermute | solution.py:26
  1699.7 6.1 collective-permute-start.3
  1701.0 4.8 collective-permute-start.4
  1709.9 4.0 collective-permute-start.5
  1714.7 6.7 collective-permute-start.3
  1716.0 5.4 collective-permute-start.4
  1725.5 3.9 collective-permute-start.5
  1730.2 6.7 collective-permute-start.3
  1731.5 5.4 collective-permute-start.4
  1741.0 3.9 collective-permute-start.5
  1745.7 6.7 collective-permute-start.3
  1747.0 5.4 collective-permute-start.4
  1761.1 6.7 collective-permute-start.3
  1762.4 5.4 collective-permute-start.4
  1776.6 6.7 collective-permute-start.3
  1777.9 5.4 collective-permute-start.4
  1792.1 8.0 collective-permute-start.3
  1793.4 6.8 collective-permute-start.4
  1809.0 8.8 collective-permute-start.3
  1810.3 7.5 collective-permute-start.4
  1826.6 8.8 collective-permute-start.3
  1827.9 7.5 collective-permute-start.4
  (10 other events, 31.9 us)
where the time goes:
time: 1860 us; the launch traced here: 1840 us
  blocking collectives  1320 us (71%)
  waiting for transfers between devices  282 us (15%)
  starting transfers between devices  145 us (8%)
  matrix products  44.2 us (2%)
  local copies, waits for them, and re-layouts  26 us (1%)
  other arithmetic  19.2 us (1%)
    psum x9, blocking collectives, forward_step(): totals = lax.psum(jnp.sum(inside, axis=(1, 2)), 'cell')  1320 us
    ppermute x18, waiting for transfers between devices, shifted(): return lax.ppermute(block, axis, route)  274 us
    ppermute x18, starting transfers between devices, extended(): before = lax.ppermute(last, axis, up)  82.4 us
    ppermute x18, starting transfers between devices, shifted(): return lax.ppermute(block, axis, route)  39.6 us
  transfers between devices with their start and end apart: 54, of which 36 were waited for; matrix products, arithmetic and copies ran while one was open for 0% of the time, Pallas kernels for 0%

commit v1 on v0

v1 whole, which is shorter than its diff:
```python
import functools

import jax
import jax.numpy as jnp
from jax import lax
from jax.experimental import pallas as pl
from jax.experimental.pallas import tpu as pltpu
from jax.sharding import PartitionSpec as P

CELL_TYPES = 16
BAND_REACH = 4
GROUP = 4
MESH = pl.DeviceIdType.MESH
F32 = jnp.float32
BF16 = jnp.bfloat16


def make_tables(rows, cols, first_block, dev_blocks, per_row, steps, table):
    slots = rows.shape[1]
    lanes = table.shape[1]
    local_row = rows - first_block
    window_col = cols - first_block + BAND_REACH
    down = lax.broadcasted_iota(jnp.int32, (slots, slots), 0)
    across = lax.broadcasted_iota(jnp.int32, (slots, slots), 1)

    def upright(line):
        return jnp.sum(jnp.where(down == across, line, 0), axis=1, keepdims=True)

    row_of, col_of = upright(local_row), upright(window_col)
    earlier = across < down
    in_col = jnp.sum(jnp.where(earlier & (window_col == col_of), 1, 0), axis=1, keepdims=True)
    in_row = jnp.sum(jnp.where(earlier & (local_row == row_of), 1, 0), axis=1, keepdims=True)
    lane = lax.broadcasted_iota(jnp.int32, (slots, lanes), 1)
    slot = lax.broadcasted_iota(jnp.int32, (slots, lanes), 0)
    named = col_of == lane
    count = jnp.sum(jnp.where(named, 1, 0), axis=0, keepdims=True)
    groups = (count + (GROUP - 1)) // GROUP
    base = jnp.sum(jnp.where(lane < col_of, groups, 0), axis=1, keepdims=True)
    place = GROUP * base + in_col
    group_of = base + in_col // GROUP
    hit = place == lane
    group_hit = group_of == lane
    before_hit = group_of == lane - 1
    here = jnp.max(jnp.where(group_hit, col_of, -1), axis=0, keepdims=True)
    before = jnp.max(jnp.where(before_hit, col_of, -2), axis=0, keepdims=True)
    row_place = per_row * row_of + in_row
    row_hit = row_place == lane
    lines = (
        jnp.sum(jnp.where(hit, slot, 0), axis=0, keepdims=True),
        jnp.sum(jnp.where(hit, row_of - dev_blocks, 0), axis=0, keepdims=True) + dev_blocks,
        jnp.where(here == before, 1, 0),
        jnp.max(jnp.where(named, group_of, 0), axis=0, keepdims=True),
        jnp.where(count > 0, 1, 0),
        jnp.sum(jnp.where(row_hit, slot, 0), axis=0, keepdims=True),
        jnp.sum(jnp.where(row_hit, col_of, 0), axis=0, keepdims=True),
        jnp.zeros_like(count),
    )
    bounds = (slots - 1, dev_blocks, 1, steps - 1, 1, slots - 1, dev_blocks + 2 * BAND_REACH - 1, 0)
    lines = [jnp.clip(line, 0, bound) for line, bound in zip(lines, bounds)]
    table[...] = jnp.concatenate(lines, axis=0)


def one_hot(labels):
    panels, side = labels.shape
    kind = lax.broadcasted_iota(jnp.int32, (panels, CELL_TYPES, side), 1)
    marks = jnp.where(labels[:, None, :] == kind, 1.0, 0.0)
    return marks.reshape(panels * CELL_TYPES, side)


def kernel(
    rows_hbm, cols_hbm, blocks_hbm, growth_hbm, first_hbm, last_hbm, mass_out, fate_out,
    rows, cols, blocks, growth, labels, table, index, scaled, window, partial, edges, own_sum, fates,
    near_sum, far_sum, whole, message, messages,
    load_sem, block_sem, index_sem, send_sem, recv_sem, all_send_sem, all_recv_sem,
):
    tm, cell = lax.axis_index("tm"), lax.axis_index("cell")
    cells = lax.axis_size("cell")
    right, left = lax.rem(cell + 1, cells), lax.rem(cell + cells - 1, cells)
    slots, side, _ = blocks.shape
    dev_blocks = scaled.shape[0] - 1
    height = scaled.shape[1]
    per_row = slots // dev_blocks
    dev_cells = dev_blocks * side
    all_cells = dev_cells * cells
    reach = BAND_REACH
    steps = partial.shape[0]
    chunks = block_sem.shape[0]
    chunk = slots // chunks

    loads = [
        pltpu.make_async_copy(rows_hbm, rows, load_sem.at[0]),
        pltpu.make_async_copy(cols_hbm, cols, load_sem.at[1]),
        pltpu.make_async_copy(growth_hbm, growth, load_sem.at[2]),
    ]
    for load in loads:
        load.start()
    first_load = pltpu.make_async_copy(first_hbm, labels.at[1], load_sem.at[3])
    last_load = pltpu.make_async_copy(last_hbm, labels.at[1], load_sem.at[3])

    @pl.when(tm == 0)
    def _():
        first_load.start()

    @pl.when(tm == 1)
    def _():
        last_load.start()

    block_loads = [
        pltpu.make_async_copy(blocks_hbm.at[0, pl.ds(i * chunk, chunk)], blocks.at[pl.ds(i * chunk, chunk)], block_sem.at[i])
        for i in range(chunks)
    ]
    for load in block_loads:
        load.start()

    barrier = pltpu.get_barrier_semaphore()

    def greet(step, carry):
        pl.semaphore_signal(barrier, inc=1, device_id=(tm, lax.rem(cell + step, cells)), device_id_type=MESH)
        return carry

    for other in (left, cell, right):
        pl.semaphore_signal(barrier, inc=1, device_id=(1 - tm, other), device_id_type=MESH)
    lax.fori_loop(1, cells, greet, 0)

    loads[0].wait()
    loads[1].wait()
    make_tables(rows[...], cols[...], cell * dev_blocks, dev_blocks, per_row, steps, table)
    index_copy = pltpu.make_async_copy(table, index, index_sem)
    index_copy.start()
    loads[2].wait()
    last_load.wait()

    def remote(source, target, number, to_tm, to_cell):
        return pltpu.make_async_remote_copy(
            src_ref=source, dst_ref=target, send_sem=send_sem.at[number], recv_sem=recv_sem.at[number],
            device_id=(to_tm, to_cell), device_id_type=MESH,
        )

    def forward():
        total = None
        for step in range(steps):
            places = [step * GROUP + i for i in range(GROUP)]
            taken = jnp.concatenate([scaled[index[1, p]] for p in places], axis=1)
            stored = jnp.concatenate([blocks[index[0, p]] for p in places], axis=0)
            product = jnp.dot(taken, stored, preferred_element_type=F32)
            if step > 0:
                product = product + jnp.where(index[2, step] > 0, total, 0.0)
            total = product
            partial[step] = total

        def column(w):
            return jnp.where(index[4, w] > 0, partial[index[3, w]], 0.0)

        row_sum = None
        for w in range(dev_blocks + 2 * reach):
            value = column(w)
            row_sum = value if row_sum is None else row_sum + value
            if w < reach:
                edges[0, w] = value.astype(BF16)
            elif w < reach + dev_blocks:
                own_sum[w - reach] = value
            else:
                edges[1, w - reach - dev_blocks] = value.astype(BF16)
        return jnp.sum(row_sum.T, axis=0, keepdims=True)

    def backward(r):
        total = None
        for k in range(0, per_row, GROUP):
            places = [r * per_row + k + i for i in range(GROUP)]
            taken = jnp.concatenate([window[index[6, p]] for p in places], axis=1)
            stored = jnp.concatenate([blocks[index[5, p]] for p in places], axis=1)
            product = lax.dot_general(taken, stored, (((1,), (1,)), ((), ())), preferred_element_type=F32)
            total = product if total is None else total + product
        grouped = total.reshape(height // CELL_TYPES, CELL_TYPES, side)
        grouped = grouped * (CELL_TYPES / jnp.sum(grouped, axis=1, keepdims=True))
        return grouped.reshape(height, side).astype(BF16)

    def tell_all():
        def tell(step, carry):
            pltpu.make_async_remote_copy(
                src_ref=message, dst_ref=messages.at[cell], send_sem=all_send_sem, recv_sem=all_recv_sem,
                device_id=(tm, lax.rem(cell + step, cells)), device_id_type=MESH,
            ).start()
            return carry

        lax.fori_loop(1, cells, tell, 0)

    def hear_all():
        heard = pltpu.make_async_remote_copy(
            src_ref=messages.at[pl.ds(0, cells - 1)], dst_ref=messages.at[pl.ds(0, cells - 1)],
            send_sem=all_send_sem, recv_sem=all_recv_sem, device_id=(tm, right), device_id_type=MESH,
        )
        heard.wait()
        messages[cell] = message[...]
        sums, units = messages[:, 0, :], messages[:, 1, :]
        largest = jnp.max(units, axis=0, keepdims=True)
        total = jnp.sum(sums * (units / largest), axis=0, keepdims=True)
        factors = [all_cells * (messages[i][1:2] / largest) / total for i in (left, cell, right)]
        square = jnp.concatenate(factors + [jnp.zeros((height - 3, height), F32)], axis=0).T
        return [square[:, i : i + 1] for i in range(3)]

    def block_range(r):
        return pl.ds(r * side, side)

    @pl.when(tm == 0)
    def _():
        scaled[dev_blocks] = jnp.zeros((height, side), BF16)
        for r in range(dev_blocks):
            marks = one_hot(labels[1, :, block_range(r)])
            scaled[r] = (marks / growth[:, block_range(r)]).astype(BF16)
        index_copy.wait()
        for load in block_loads:
            load.wait()
        sums = forward()
        message[...] = jnp.concatenate([sums, jnp.ones_like(sums)], axis=0)
        pl.semaphore_wait(barrier, cells - 1 + 3)
        to_left = remote(edges.at[0], near_sum.at[1], 0, 1, left)
        to_right = remote(edges.at[1], near_sum.at[0], 1, 1, right)
        to_other = remote(own_sum, whole, 2, 1, cell)
        to_left.start()
        to_right.start()
        to_other.start()
        tell_all()
        remote(fates, window.at[pl.ds(0, reach)], 3, 1, left).wait_recv()
        remote(fates, window.at[pl.ds(reach, dev_blocks)], 4, 1, cell).wait_recv()
        remote(fates, window.at[pl.ds(reach + dev_blocks, reach)], 5, 1, right).wait_recv()
        for r in range(dev_blocks):
            fate_out[0, :, block_range(r)] = backward(r)
        remote(whole, whole, 6, 1, cell).wait_recv()
        factor = hear_all()[1]
        for r in range(dev_blocks):
            mass_out[0, :, block_range(r)] = (whole[r] * factor).astype(BF16)
        to_left.wait_send()
        to_right.wait_send()
        to_other.wait_send()

    @pl.when(tm == 1)
    def _():
        pl.semaphore_wait(barrier, cells - 1 + 3)
        labels_right = remote(labels.at[1], labels.at[0], 7, 1, right)
        labels_left = remote(labels.at[1], labels.at[2], 8, 1, left)
        labels_right.start()
        labels_left.start()
        for r in range(dev_blocks):
            window[reach + r] = one_hot(labels[1, :, block_range(r)]).astype(BF16)
        index_copy.wait()
        for load in block_loads:
            load.wait()
        labels_right.wait_recv()
        labels_left.wait_recv()
        for r in range(reach):
            window[r] = one_hot(labels[0, :, block_range(dev_blocks - reach + r)]).astype(BF16)
            window[reach + dev_blocks + r] = one_hot(labels[2, :, block_range(r)]).astype(BF16)
        for r in range(dev_blocks):
            value = backward(r)
            fates[r] = value
            fate_out[0, :, block_range(r)] = value
        fate_right = remote(fates, window.at[pl.ds(0, reach)], 3, 0, right)
        fate_here = remote(fates, window.at[pl.ds(reach, dev_blocks)], 4, 0, cell)
        fate_left = remote(fates, window.at[pl.ds(reach + dev_blocks, reach)], 5, 0, left)
        fate_right.start()
        fate_left.start()
        fate_here.start()

        remote(edges.at[0], near_sum.at[1], 0, 0, right).wait_recv()
        remote(edges.at[1], near_sum.at[0], 1, 0, left).wait_recv()
        remote(own_sum, whole, 2, 0, cell).wait_recv()
        row_sum = jnp.zeros((height, side), F32)
        for r in range(dev_blocks):
            value = whole[r] + near_sum[0, r].astype(F32) + near_sum[1, r].astype(F32)
            whole[r] = value
            row_sum = row_sum + value
        mass_back = remote(whole, whole, 6, 0, cell)
        mass_back.start()
        mean = jnp.sum(row_sum, axis=1, keepdims=True) * (1.0 / dev_cells)
        unit = jnp.where(mean > 0.0, mean, 1.0)
        unit = jnp.broadcast_to(unit, (height, side))
        scaled[dev_blocks] = jnp.zeros((height, side), BF16)
        for r in range(dev_blocks):
            scaled[r] = (whole[r] / unit / growth[:, block_range(r)]).astype(BF16)
        sums = forward()
        message[...] = jnp.concatenate([sums, unit.T[0:1]], axis=0)
        to_left = remote(edges.at[0], far_sum.at[1], 9, 1, left)
        to_right = remote(edges.at[1], far_sum.at[0], 10, 1, right)
        to_left.start()
        to_right.start()
        tell_all()
        to_left.wait_recv()
        to_right.wait_recv()
        factors = hear_all()
        for r in range(dev_blocks):
            value = own_sum[r] * factors[1] + far_sum[0, r].astype(F32) * factors[0] + far_sum[1, r].astype(F32) * factors[2]
            mass_out[0, :, block_range(r)] = value.astype(BF16)
        for copy in (labels_right, labels_left, fate_right, fate_here, fate_left, mass_back, to_left, to_right):
            copy.wait_send()


def on_device(block_rows, block_cols, block_values, growth, first_labels, last_labels):
    slots, side = block_values.shape[1], block_values.shape[2]
    dev_cells = growth.shape[1]
    dev_blocks = dev_cells // side
    panels = first_labels.shape[0]
    height = panels * CELL_TYPES
    cells = lax.axis_size("cell")
    columns = dev_blocks + 2 * BAND_REACH
    steps = (slots + (GROUP - 1) * columns) // GROUP
    out = jax.ShapeDtypeStruct((1, height, dev_cells), BF16)
    copies = 11
    return pl.pallas_call(
        kernel,
        out_shape=(out, out),
        in_specs=[pl.BlockSpec(memory_space=pl.ANY)] * 6,
        out_specs=(pl.BlockSpec(memory_space=pltpu.VMEM), pl.BlockSpec(memory_space=pltpu.VMEM)),
        scratch_shapes=[
            pltpu.VMEM((1, slots), jnp.int32),
            pltpu.VMEM((1, slots), jnp.int32),
            pltpu.VMEM((slots, side, side), BF16),
            pltpu.VMEM((1, dev_cells), F32),
            pltpu.VMEM((3, panels, dev_cells), jnp.int32),
            pltpu.VMEM((8, 128), jnp.int32),
            pltpu.SMEM((8, 128), jnp.int32),
            pltpu.VMEM((dev_blocks + 1, height, side), BF16),
            pltpu.VMEM((columns, height, side), BF16),
            pltpu.VMEM((steps, height, side), F32),
            pltpu.VMEM((2, BAND_REACH, height, side), BF16),
            pltpu.VMEM((dev_blocks, height, side), F32),
            pltpu.VMEM((dev_blocks, height, side), BF16),
            pltpu.VMEM((2, BAND_REACH, height, side), BF16),
            pltpu.VMEM((2, BAND_REACH, height, side), BF16),
            pltpu.VMEM((dev_blocks, height, side), F32),
            pltpu.VMEM((2, height), F32),
            pltpu.VMEM((cells, 2, height), F32),
            pltpu.SemaphoreType.DMA((4,)),
            pltpu.SemaphoreType.DMA((4,)),
            pltpu.SemaphoreType.DMA,
            pltpu.SemaphoreType.DMA((copies,)),
            pltpu.SemaphoreType.DMA((copies,)),
            pltpu.SemaphoreType.DMA,
            pltpu.SemaphoreType.DMA,
        ],
        compiler_params=pltpu.CompilerParams(collective_id=0, has_side_effects=True, vmem_limit_bytes=40 * 1024 * 1024),
    )(block_rows, block_cols, block_values, growth, first_labels, last_labels)


def solution(mesh):
    placed = (
        P("tm", "cell"),
        P("tm", "cell"),
        P("tm", "cell", None, None),
        P("tm", "cell"),
        P(None, "cell"),
        P(None, "cell"),
    )
    return jax.shard_map(
        on_device,
        mesh=mesh,
        in_specs=placed,
        out_specs=(P("tm", None, "cell"), P("tm", None, "cell")),
        check_vma=False,
    )
```

time: 1860 us -> 32.3 us (0.02)
  blocking collectives: 1320 us -> 0 us
  waiting for transfers between devices: 282 us -> 0 us
  starting transfers between devices: 145 us -> 0 us
  matrix products: 44.2 us -> 0 us
  Pallas kernels: 0 us -> 25.1 us
  local copies, waits for them, and re-layouts: 26 us -> 6.32 us
  other arithmetic: 19.2 us -> 0 us
    psum x9 -> x0, blocking collectives: 1320 us -> none  [forward_step(): totals = lax.psum(jnp.sum(inside, axis=(1, 2)), 'cell')]
    ppermute x54 -> x0, waiting for transfers between devices: 282 us -> none  [the longest x18 274 us: shifted(): return lax.ppermute(block, axis, route)]
    ppermute x54 -> x0, starting transfers between devices: 145 us -> none  [the longest x18 82.4 us: extended(): before = lax.ppermute(last, axis, up)]
    dot_general x18 -> x0, matrix products: 44.2 us -> none  [the longest x9 25 us: backward_step(): jnp.einsum('skl,sql->sqk', blocks, picked, preferred_element_type=jnp.flo...]
    pallas_call x0 -> x1, Pallas kernels: none -> 25.1 us  [on_device(): pl.pallas_call(kernel, out_shape=(out, out), in_specs=[pl.BlockSpec(memor...]
  transfers between devices with their start and end apart: 54 -> 0, of which waited for: 36 -> 0; matrix products, arithmetic and copies ran while one was open for 0% -> 0% of each run, Pallas kernels for 0% -> 0%
where the time goes in v1:
time: 32.3 us; the launch traced here: 32 us
  Pallas kernels  25.1 us (78%)
  local copies, waits for them, and re-layouts  6.32 us (20%)
  between operations  0.65 us (2%)
    pallas_call x1, Pallas kernels, on_device(): pl.pallas_call(kernel, out_shape=(out, out), in_specs=[pl.BlockSpec(memor...  25.1 us
    unnamed x14, local copies, waits for them, and re-layouts  6.32 us

profile of v1, /device:TPU:1, one launch (start us, length us, event | category | flops | bytes accessed | tf_op | source)
XLA Modules:
  0.0 32.0 jit_solution(14241579174041103527)
XLA Ops:
  0.6 0.0 copy-start
  0.6 1.6 %copy-done = bf16[1,64,128,128]{3,2,1,0:T(8,128)(2,1)S(1)} copy-done((bf16[1,64,128,128]{3,2,1,0:T(8,128)(2,1)S(1)}, bf16[1,64,128,128]{3,2,1,0:T(8,128)(2,1)}, u32[]{:S(2)}) %copy-start) | copy-done | bytes 2097176
  2.2 0.0 copy-start.1
  2.2 0.7 %copy-done.1 = s32[8,512]{1,0:T(8,128)S(1)} copy-done((s32[8,512]{1,0:T(8,128)S(1)}, s32[8,512]{1,0:T(8,128)}, u32[]{:S(2)}) %copy-start.1) | copy-done | bytes 16408
  2.9 0.0 copy-start.2
  2.9 0.7 %copy-done.2 = s32[8,512]{1,0:T(8,128)S(1)} copy-done((s32[8,512]{1,0:T(8,128)S(1)}, s32[8,512]{1,0:T(8,128)}, u32[]{:S(2)}) %copy-start.2) | copy-done | bytes 16408
  3.7 0.0 copy-start.3
  3.7 0.7 %copy-done.3 = f32[1,512]{1,0:T(1,128)S(1)} copy-done((f32[1,512]{1,0:T(1,128)S(1)}, f32[1,512]{1,0:T(1,128)}, u32[]{:S(2)}) %copy-start.3) | copy-done | bytes 2072
  4.3 0.0 copy-start.4
  4.3 0.7 %copy-done.4 = s32[1,64]{1,0:T(1,128)S(1)} copy-done((s32[1,64]{1,0:T(1,128)S(1)}, s32[1,64]{1,0:T(1,128)}, u32[]{:S(2)}) %copy-start.4) | copy-done | bytes 280
  5.0 0.0 copy-start.5
  5.0 0.7 %copy-done.5 = s32[1,64]{1,0:T(1,128)S(1)} copy-done((s32[1,64]{1,0:T(1,128)S(1)}, s32[1,64]{1,0:T(1,128)}, u32[]{:S(2)}) %copy-start.5) | copy-done | bytes 280
  5.7 25.1 %shard_map.77 = (bf16[1,128,512]{2,1,0:T(8,128)(2,1)S(1)}, bf16[1,128,512]{2,1,0:T(8,128)(2,1)S(1)}) custom-call(s32[1,64]{1,0:T(1,128)S(1)} %copy-done.4, s32[1,64]{1,0:T(1,128)S(1)} %copy-done.5, bf16[1,64,128,128]{3,2,1,0:T(8,128)(2,1)S(1)} %copy-done, f32[1,512]{1,0:T(1,128)S(1)} %copy-done.3, s32[8,512]{1,0:T(8,128)S(1)} %copy-done.1, ...), custom_call_target="tpu_custom_call" | custom-call | tf_op jit(solution)/shard_map/pallas_call | solution.py:309
  30.7 0.7 %copy.10 = bf16[1,128,512]{2,1,0:T(8,128)(2,1)} copy(bf16[1,128,512]{2,1,0:T(8,128)(2,1)S(1)} %get-tuple-element.4) | data formatting | bytes 262144
  31.4 0.7 %copy.11 = bf16[1,128,512]{2,1,0:T(8,128)(2,1)} copy(bf16[1,128,512]{2,1,0:T(8,128)(2,1)S(1)} %get-tuple-element.5) | data formatting | bytes 262144
Async XLA Ops:
  0.6 1.6 %copy-start = (bf16[1,64,128,128]{3,2,1,0:T(8,128)(2,1)S(1)}, bf16[1,64,128,128]{3,2,1,0:T(8,128)(2,1)}, u32[]{:S(2)}) copy-start(bf16[1,64,128,128]{3,2,1,0:T(8,128)(2,1)} %blocks_hbm.1) | copy-start | bytes 6291460
  2.2 0.7 %copy-start.1 = (s32[8,512]{1,0:T(8,128)S(1)}, s32[8,512]{1,0:T(8,128)}, u32[]{:S(2)}) copy-start(s32[8,512]{1,0:T(8,128)} %first_hbm.1) | copy-start | bytes 49156
  2.9 0.7 %copy-start.2 = (s32[8,512]{1,0:T(8,128)S(1)}, s32[8,512]{1,0:T(8,128)}, u32[]{:S(2)}) copy-start(s32[8,512]{1,0:T(8,128)} %last_hbm.1) | copy-start | bytes 49156
  3.7 0.7 %copy-start.3 = (f32[1,512]{1,0:T(1,128)S(1)}, f32[1,512]{1,0:T(1,128)}, u32[]{:S(2)}) copy-start(f32[1,512]{1,0:T(1,128)} %growth_hbm.1) | copy-start | bytes 6148
  4.3 0.7 %copy-start.4 = (s32[1,64]{1,0:T(1,128)S(1)}, s32[1,64]{1,0:T(1,128)}, u32[]{:S(2)}) copy-start(s32[1,64]{1,0:T(1,128)} %rows_hbm.1) | copy-start | bytes 772
  5.0 0.7 %copy-start.5 = (s32[1,64]{1,0:T(1,128)S(1)}, s32[1,64]{1,0:T(1,128)}, u32[]{:S(2)}) copy-start(s32[1,64]{1,0:T(1,128)} %cols_hbm.1) | copy-start | bytes 772

commit v2 on v1

v2 whole, which is shorter than its diff:
```python
import functools

import jax
import jax.numpy as jnp
from jax import lax
from jax.experimental import pallas as pl
from jax.experimental.pallas import tpu as pltpu
from jax.sharding import PartitionSpec as P

CELL_TYPES = 16
BAND_REACH = 4
GROUP = 4
MESH = pl.DeviceIdType.MESH
F32 = jnp.float32
BF16 = jnp.bfloat16


def make_tables(rows, cols, first_block, dev_blocks, per_row, steps, table):
    slots = rows.shape[1]
    lanes = table.shape[1]
    local_row = rows - first_block
    window_col = cols - first_block + BAND_REACH
    down = lax.broadcasted_iota(jnp.int32, (slots, slots), 0)
    across = lax.broadcasted_iota(jnp.int32, (slots, slots), 1)

    def upright(line):
        return jnp.sum(jnp.where(down == across, line, 0), axis=1, keepdims=True)

    row_of, col_of = upright(local_row), upright(window_col)
    earlier = across < down
    in_col = jnp.sum(jnp.where(earlier & (window_col == col_of), 1, 0), axis=1, keepdims=True)
    in_row = jnp.sum(jnp.where(earlier & (local_row == row_of), 1, 0), axis=1, keepdims=True)
    lane = lax.broadcasted_iota(jnp.int32, (slots, lanes), 1)
    slot = lax.broadcasted_iota(jnp.int32, (slots, lanes), 0)
    named = col_of == lane
    count = jnp.sum(jnp.where(named, 1, 0), axis=0, keepdims=True)
    groups = (count + (GROUP - 1)) // GROUP
    base = jnp.sum(jnp.where(lane < col_of, groups, 0), axis=1, keepdims=True)
    place = GROUP * base + in_col
    group_of = base + in_col // GROUP
    hit = place == lane
    group_hit = group_of == lane
    before_hit = group_of == lane - 1
    here = jnp.max(jnp.where(group_hit, col_of, -1), axis=0, keepdims=True)
    before = jnp.max(jnp.where(before_hit, col_of, -2), axis=0, keepdims=True)
    row_place = per_row * row_of + in_row
    row_hit = row_place == lane
    lines = (
        jnp.sum(jnp.where(hit, slot, 0), axis=0, keepdims=True),
        jnp.sum(jnp.where(hit, row_of - dev_blocks, 0), axis=0, keepdims=True) + dev_blocks,
        jnp.where(here == before, 1, 0),
        jnp.max(jnp.where(named, group_of, 0), axis=0, keepdims=True),
        jnp.where(count > 0, 1, 0),
        jnp.sum(jnp.where(row_hit, slot, 0), axis=0, keepdims=True),
        jnp.sum(jnp.where(row_hit, col_of, 0), axis=0, keepdims=True),
        jnp.zeros_like(count),
    )
    bounds = (slots - 1, dev_blocks, 1, steps - 1, 1, slots - 1, dev_blocks + 2 * BAND_REACH - 1, 0)
    lines = [jnp.clip(line, 0, bound) for line, bound in zip(lines, bounds)]
    table[...] = jnp.concatenate(lines, axis=0)


def one_hot(labels):
    panels, side = labels.shape
    kind = lax.broadcasted_iota(jnp.int32, (panels, CELL_TYPES, side), 1)
    marks = jnp.where(labels[:, None, :] == kind, 1.0, 0.0)
    return marks.reshape(panels * CELL_TYPES, side)


def kernel(
    rows_hbm, cols_hbm, blocks_hbm, growth_hbm, first_hbm, last_hbm, mass_out, fate_out,
    rows, cols, blocks, growth, labels, table, index, scaled, window, partial, edges, own_sum, fates,
    near_sum, far_sum, whole, first_total, first_factor, message, messages,
    load_sem, block_sem, index_sem, send_sem, recv_sem, all_send_sem, all_recv_sem,
):
    tm, cell = lax.axis_index("tm"), lax.axis_index("cell")
    cells = lax.axis_size("cell")
    right, left = lax.rem(cell + 1, cells), lax.rem(cell + cells - 1, cells)
    has_right, has_left = cell < cells - 1, cell > 0
    slots, side, _ = blocks.shape
    dev_blocks = scaled.shape[0] - 1
    height = scaled.shape[1]
    per_row = slots // dev_blocks
    dev_cells = dev_blocks * side
    all_cells = dev_cells * cells
    reach = BAND_REACH
    steps = partial.shape[0]
    chunks = block_sem.shape[0]
    chunk = slots // chunks

    load_rows = pltpu.make_async_copy(rows_hbm, rows, load_sem.at[0])
    load_cols = pltpu.make_async_copy(cols_hbm, cols, load_sem.at[1])
    load_growth = pltpu.make_async_copy(growth_hbm, growth, load_sem.at[2])
    load_first = pltpu.make_async_copy(first_hbm, labels.at[1], load_sem.at[3])
    load_last = pltpu.make_async_copy(last_hbm, labels.at[1], load_sem.at[3])
    load_passed = pltpu.make_async_copy(last_hbm, labels.at[0], load_sem.at[4])
    load_blocks = [
        pltpu.make_async_copy(blocks_hbm.at[0, pl.ds(i * chunk, chunk)], blocks.at[pl.ds(i * chunk, chunk)], block_sem.at[i])
        for i in range(chunks)
    ]
    barrier = pltpu.get_barrier_semaphore()

    def greet(to_tm, to_cell):
        pl.semaphore_signal(barrier, inc=1, device_id=(to_tm, to_cell), device_id_type=MESH)

    load_rows.start()
    load_cols.start()
    for load in load_blocks:
        load.start()
    load_growth.start()

    @pl.when(tm == 0)
    def _():
        load_first.start()
        load_passed.start()

    @pl.when(tm == 1)
    def _():
        load_last.start()
        greet(0, cell)

        @pl.when(has_left)
        def _():
            greet(0, left)

        @pl.when(has_right)
        def _():
            greet(0, right)

        def greet_all(step, carry):
            greet(1, lax.rem(cell + step, cells))
            return carry

        lax.fori_loop(1, cells, greet_all, 0)

    load_rows.wait()
    load_cols.wait()
    make_tables(rows[...], cols[...], cell * dev_blocks, dev_blocks, per_row, steps, table)
    index_copy = pltpu.make_async_copy(table, index, index_sem)
    index_copy.start()

    def remote(source, target, number, to_tm, to_cell):
        return pltpu.make_async_remote_copy(
            src_ref=source, dst_ref=target, send_sem=send_sem.at[number], recv_sem=recv_sem.at[number],
            device_id=(to_tm, to_cell), device_id_type=MESH,
        )

    def block_range(r):
        return pl.ds(r * side, side)

    def column_sums(beside=None):
        total = None
        for step in range(steps):
            places = [step * GROUP + i for i in range(GROUP)]
            taken = jnp.concatenate([scaled[index[1, p]] for p in places], axis=1)
            stored = jnp.concatenate([blocks[index[0, p]] for p in places], axis=0)
            product = jnp.dot(taken, stored, preferred_element_type=F32)
            if step > 0:
                product = product + jnp.where(index[2, step] > 0, total, 0.0)
            total = product
            partial[step] = total
            if beside is not None:
                beside(step)

    def column(w):
        return jnp.where(index[4, w] > 0, partial[index[3, w]], 0.0)

    def outer_columns():
        for w in range(reach):
            edges[0, w] = column(w).astype(BF16)
            edges[1, w] = column(reach + dev_blocks + w).astype(BF16)

    def own_columns():
        for w in range(dev_blocks):
            own_sum[w] = column(reach + w)

    def fate_block(r):
        total = None
        for k in range(0, per_row, GROUP):
            places = [r * per_row + k + i for i in range(GROUP)]
            taken = jnp.concatenate([window[index[6, p]] for p in places], axis=1)
            stored = jnp.concatenate([blocks[index[5, p]] for p in places], axis=1)
            product = lax.dot_general(taken, stored, (((1,), (1,)), ((), ())), preferred_element_type=F32)
            total = product if total is None else total + product
        grouped = total.reshape(height // CELL_TYPES, CELL_TYPES, side)
        grouped = grouped * (CELL_TYPES / jnp.sum(grouped, axis=1, keepdims=True))
        return grouped.reshape(height, side).astype(BF16)

    def row_totals(r):
        ones = jnp.ones((8, GROUP * side), BF16)
        total = None
        for k in range(0, per_row, GROUP):
            places = [r * per_row + k + i for i in range(GROUP)]
            stored = jnp.concatenate([blocks[index[5, p]] for p in places], axis=1)
            product = lax.dot_general(ones, stored, (((1,), (1,)), ((), ())), preferred_element_type=F32)
            total = product if total is None else total + product
        return total[0:1]

    @pl.when(tm == 0)
    def _():
        scaled[dev_blocks] = jnp.zeros((height, side), BF16)
        load_growth.wait()
        load_first.wait()
        for r in range(dev_blocks):
            marks = one_hot(labels[1, :, block_range(r)])
            scaled[r] = (marks / growth[:, block_range(r)]).astype(BF16)
        index_copy.wait()
        for load in load_blocks:
            load.wait()
        column_sums()
        outer_columns()
        load_passed.wait()
        labels_right = remote(labels.at[0], labels.at[0], 7, 1, right)
        labels_left = remote(labels.at[0], labels.at[2], 8, 1, left)
        edge_left = remote(edges.at[0], near_sum.at[1], 0, 1, left)
        edge_right = remote(edges.at[1], near_sum.at[0], 1, 1, right)
        own_here = remote(own_sum, whole, 2, 1, cell)
        total_here = remote(first_total, first_total, 11, 1, cell)
        pl.semaphore_wait(barrier, 2 + lax.div(cell + cells - 1, cells) - lax.div(cell + 1, cells))

        @pl.when(has_right)
        def _():
            edge_right.start()
            labels_right.start()

        @pl.when(has_left)
        def _():
            edge_left.start()
            labels_left.start()

        own_columns()
        own_here.start()
        row_sum = own_sum[0]
        for w in range(1, dev_blocks):
            row_sum = row_sum + own_sum[w]
        for w in range(reach):
            row_sum = row_sum + column(w) + column(reach + dev_blocks + w)
        first_total[...] = jnp.sum(row_sum.T, axis=0, keepdims=True)
        total_here.start()

        @pl.when(has_left)
        def _():
            remote(fates, window.at[pl.ds(0, reach)], 3, 1, left).wait_recv()

        @pl.when(has_right)
        def _():
            remote(fates, window.at[pl.ds(reach + dev_blocks, reach)], 5, 1, right).wait_recv()

        remote(fates, window.at[pl.ds(reach, dev_blocks)], 4, 1, cell).wait_recv()
        for r in range(dev_blocks):
            fate_out[0, :, block_range(r)] = fate_block(r)

        @pl.when(has_right)
        def _():
            edge_right.wait_send()
            labels_right.wait_send()

        @pl.when(has_left)
        def _():
            edge_left.wait_send()
            labels_left.wait_send()

        own_here.wait_send()
        total_here.wait_send()
        remote(whole, whole, 6, 1, cell).wait_recv()
        remote(first_factor, first_factor, 12, 1, cell).wait_recv()
        factor = jnp.broadcast_to(first_factor[...], (height, height)).T
        for r in range(dev_blocks):
            mass_out[0, :, block_range(r)] = (whole[r] * factor).astype(BF16)

    @pl.when(tm == 1)
    def _():
        load_last.wait()
        for r in range(dev_blocks):
            window[reach + r] = one_hot(labels[1, :, block_range(r)]).astype(BF16)
        index_copy.wait()
        for load in load_blocks:
            load.wait()
        totals = [row_totals(r) for r in range(dev_blocks)]
        scaled[dev_blocks] = jnp.zeros((height, side), BF16)
        load_growth.wait()

        @pl.when(has_left)
        def _():
            remote(labels.at[0], labels.at[0], 7, 0, left).wait_recv()
            for r in range(reach):
                window[r] = one_hot(labels[0, :, block_range(dev_blocks - reach + r)]).astype(BF16)

        @pl.when(has_right)
        def _():
            remote(labels.at[0], labels.at[2], 8, 0, right).wait_recv()
            for r in range(reach):
                window[reach + dev_blocks + r] = one_hot(labels[2, :, block_range(r)]).astype(BF16)

        for r in range(dev_blocks):
            value = fate_block(r)
            fates[r] = value
            fate_out[0, :, block_range(r)] = value
        remote(own_sum, whole, 2, 0, cell).wait_recv()
        fate_right = remote(fates, window.at[pl.ds(0, reach)], 3, 0, right)
        fate_here = remote(fates, window.at[pl.ds(reach, dev_blocks)], 4, 0, cell)
        fate_left = remote(fates, window.at[pl.ds(reach + dev_blocks, reach)], 5, 0, left)

        @pl.when(has_right)
        def _():
            fate_right.start()

        @pl.when(has_left)
        def _():
            fate_left.start()

        fate_here.start()

        @pl.when(has_right)
        def _():
            remote(edges.at[0], near_sum.at[1], 0, 0, right).wait_recv()

        @pl.when(has_left)
        def _():
            remote(edges.at[1], near_sum.at[0], 1, 0, left).wait_recv()

        @pl.when(jnp.logical_not(has_right))
        def _():
            near_sum[1] = jnp.zeros(near_sum.shape[1:], BF16)
            far_sum[1] = jnp.zeros(far_sum.shape[1:], BF16)

        @pl.when(jnp.logical_not(has_left))
        def _():
            near_sum[0] = jnp.zeros(near_sum.shape[1:], BF16)
            far_sum[0] = jnp.zeros(far_sum.shape[1:], BF16)

        row_sum = jnp.zeros((height, side), F32)
        for r in range(dev_blocks):
            value = whole[r] + near_sum[0, r].astype(F32) + near_sum[1, r].astype(F32)
            whole[r] = value
            row_sum = row_sum + value
        whole_back = remote(whole, whole, 6, 0, cell)
        whole_back.start()
        mean = jnp.sum(row_sum, axis=1, keepdims=True) * (1.0 / dev_cells)
        unit = jnp.broadcast_to(jnp.where(mean > 0.0, mean, 1.0), (height, side))
        weighted = jnp.zeros((height, side), F32)
        for r in range(dev_blocks):
            value = (whole[r] / unit / growth[:, block_range(r)]).astype(BF16)
            scaled[r] = value
            weighted = weighted + value.astype(F32) * totals[r]
        remote(first_total, first_total, 11, 0, cell).wait_recv()
        message[...] = jnp.concatenate([jnp.sum(weighted.T, axis=0, keepdims=True), unit.T[0:1], first_total[...], first_total[...]], axis=0)
        pl.semaphore_wait(barrier, cells - 1)

        def tell(step):
            pltpu.make_async_remote_copy(
                src_ref=message, dst_ref=messages.at[cell], send_sem=all_send_sem, recv_sem=all_recv_sem,
                device_id=(1, lax.rem(cell + step, cells)), device_id_type=MESH,
            ).start()

        share = -(-(cells - 1) // steps)

        def tell_some(step):
            for number in range(1 + step * share, min(1 + (step + 1) * share, cells)):
                tell(number)

        column_sums(tell_some)
        outer_columns()
        far_left = remote(edges.at[0], far_sum.at[1], 9, 1, left)
        far_right = remote(edges.at[1], far_sum.at[0], 10, 1, right)

        @pl.when(has_right)
        def _():
            far_right.start()

        @pl.when(has_left)
        def _():
            far_left.start()

        own_columns()
        heard = pltpu.make_async_remote_copy(
            src_ref=messages.at[pl.ds(0, cells - 1)], dst_ref=messages.at[pl.ds(0, cells - 1)],
            send_sem=all_send_sem, recv_sem=all_recv_sem, device_id=(1, lax.rem(cell + 1, cells)), device_id_type=MESH,
        )
        heard.wait()
        messages[cell] = message[...]
        first_factor[...] = all_cells / jnp.sum(messages[:, 2, :], axis=0, keepdims=True)
        factor_here = remote(first_factor, first_factor, 12, 0, cell)
        factor_here.start()
        sums, units = messages[:, 0, :], messages[:, 1, :]
        largest = jnp.max(units, axis=0, keepdims=True)
        total = jnp.sum(sums * (units / largest), axis=0, keepdims=True)
        sources = (left, cell, right)
        factors = [all_cells * (messages[i][1:2] / largest) / total for i in sources]
        square = jnp.concatenate(factors + [jnp.zeros((height - 3, height), F32)], axis=0).T
        factors = [square[:, i : i + 1] for i in range(3)]

        @pl.when(has_left)
        def _():
            remote(edges.at[1], far_sum.at[0], 10, 1, left).wait_recv()

        @pl.when(has_right)
        def _():
            remote(edges.at[0], far_sum.at[1], 9, 1, right).wait_recv()

        for r in range(dev_blocks):
            value = own_sum[r] * factors[1] + far_sum[0, r].astype(F32) * factors[0] + far_sum[1, r].astype(F32) * factors[2]
            mass_out[0, :, block_range(r)] = value.astype(BF16)

        @pl.when(has_right)
        def _():
            fate_right.wait_send()
            far_right.wait_send()

        @pl.when(has_left)
        def _():
            fate_left.wait_send()
            far_left.wait_send()

        fate_here.wait_send()
        whole_back.wait_send()
        factor_here.wait_send()


def on_device(block_rows, block_cols, block_values, growth, first_labels, last_labels):
    slots, side = block_values.shape[1], block_values.shape[2]
    dev_cells = growth.shape[1]
    dev_blocks = dev_cells // side
    panels = first_labels.shape[0]
    height = panels * CELL_TYPES
    cells = lax.axis_size("cell")
    columns = dev_blocks + 2 * BAND_REACH
    steps = (slots + (GROUP - 1) * columns) // GROUP
    out = jax.ShapeDtypeStruct((1, height, dev_cells), BF16)
    copies = 13
    return pl.pallas_call(
        kernel,
        out_shape=(out, out),
        in_specs=[pl.BlockSpec(memory_space=pl.ANY)] * 6,
        out_specs=(pl.BlockSpec(memory_space=pltpu.VMEM), pl.BlockSpec(memory_space=pltpu.VMEM)),
        scratch_shapes=[
            pltpu.VMEM((1, slots), jnp.int32),
            pltpu.VMEM((1, slots), jnp.int32),
            pltpu.VMEM((slots, side, side), BF16),
            pltpu.VMEM((1, dev_cells), F32),
            pltpu.VMEM((3, panels, dev_cells), jnp.int32),
            pltpu.VMEM((8, 128), jnp.int32),
            pltpu.SMEM((8, 128), jnp.int32),
            pltpu.VMEM((dev_blocks + 1, height, side), BF16),
            pltpu.VMEM((columns, height, side), BF16),
            pltpu.VMEM((steps, height, side), F32),
            pltpu.VMEM((2, BAND_REACH, height, side), BF16),
            pltpu.VMEM((dev_blocks, height, side), F32),
            pltpu.VMEM((dev_blocks, height, side), BF16),
            pltpu.VMEM((2, BAND_REACH, height, side), BF16),
            pltpu.VMEM((2, BAND_REACH, height, side), BF16),
            pltpu.VMEM((dev_blocks, height, side), F32),
            pltpu.VMEM((1, height), F32),
            pltpu.VMEM((1, height), F32),
            pltpu.VMEM((4, height), F32),
            pltpu.VMEM((cells, 4, height), F32),
            pltpu.SemaphoreType.DMA((5,)),
            pltpu.SemaphoreType.DMA((4,)),
            pltpu.SemaphoreType.DMA,
            pltpu.SemaphoreType.DMA((copies,)),
            pltpu.SemaphoreType.DMA((copies,)),
            pltpu.SemaphoreType.DMA,
            pltpu.SemaphoreType.DMA,
        ],
        compiler_params=pltpu.CompilerParams(collective_id=0, has_side_effects=True, vmem_limit_bytes=40 * 1024 * 1024),
    )(*[pltpu.with_memory_space_constraint(x, pltpu.HBM) for x in (block_rows, block_cols, block_values, growth, first_labels, last_labels)])


def solution(mesh):
    placed = (
        P("tm", "cell"),
        P("tm", "cell"),
        P("tm", "cell", None, None),
        P("tm", "cell"),
        P(None, "cell"),
        P(None, "cell"),
    )
    return jax.shard_map(
        on_device,
        mesh=mesh,
        in_specs=placed,
        out_specs=(P("tm", None, "cell"), P("tm", None, "cell")),
        check_vma=False,
    )
```

time: 32.3 us -> 24.8 us (0.77)
  local copies, waits for them, and re-layouts: 6.32 us -> 1.31 us
  Pallas kernels: 25.1 us -> 22.7 us
    unnamed x14 -> x2, local copies, waits for them, and re-layouts: 6.32 us -> 1.31 us
    pallas_call x1, Pallas kernels: 25.1 us -> 22.7 us  [on_device(): pl.pallas_call(kernel, out_shape=(out, out), in_specs=[pl.BlockSpec(memor...]
where the time goes in v2:
time: 24.8 us; the launch traced here: 24.6 us
  Pallas kernels  22.7 us (92%)
  local copies, waits for them, and re-layouts  1.31 us (5%)
  between operations  0.64 us (3%)
    pallas_call x1, Pallas kernels, on_device(): pl.pallas_call(kernel, out_shape=(out, out), in_specs=[pl.BlockSpec(memor...  22.7 us
    unnamed x2, local copies, waits for them, and re-layouts  1.31 us

profile of v2, /device:TPU:1, one launch (start us, length us, event | category | flops | bytes accessed | tf_op | source)
XLA Modules:
  0.0 24.6 jit_solution(18181892262319218167)
XLA Ops:
  0.6 22.7 %shard_map.77 = (bf16[1,128,512]{2,1,0:T(8,128)(2,1)S(1)}, bf16[1,128,512]{2,1,0:T(8,128)(2,1)S(1)}) custom-call(s32[1,64]{1,0:T(1,128)} %rows_hbm.1, s32[1,64]{1,0:T(1,128)} %cols_hbm.1, bf16[1,64,128,128]{3,2,1,0:T(8,128)(2,1)} %blocks_hbm.1, f32[1,512]{1,0:T(1,128)} %growth_hbm.1, s32[8,512]{1,0:T(8,128)} %first_hbm.1, s32[8,512]{1,0:T(8,128)} %last_hbm.1), custom_call_target="tpu_custom_call" | custom-call | tf_op jit(solution)/shard_map/pallas_call | solution.py:431
  23.3 0.7 %copy.10 = bf16[1,128,512]{2,1,0:T(8,128)(2,1)} copy(bf16[1,128,512]{2,1,0:T(8,128)(2,1)S(1)} %get-tuple-element.4) | data formatting | bytes 262144
  24.0 0.7 %copy.11 = bf16[1,128,512]{2,1,0:T(8,128)(2,1)} copy(bf16[1,128,512]{2,1,0:T(8,128)(2,1)S(1)} %get-tuple-element.5) | data formatting | bytes 262144

commit v3 on v2

--- a/solution.py
+++ b/solution.py
@@ -69,7 +69,7 @@
 
 def kernel(
     rows_hbm, cols_hbm, blocks_hbm, growth_hbm, first_hbm, last_hbm, mass_out, fate_out,
-    rows, cols, blocks, growth, labels, table, index, scaled, window, partial, edges, own_sum, fates,
+    rows, cols, blocks, growth, per_growth, labels, table, index, scaled, window, partial, edges, own_sum, fates,
     near_sum, far_sum, whole, first_total, first_factor, message, messages,
     load_sem, block_sem, index_sem, send_sem, recv_sem, all_send_sem, all_recv_sem,
 ):
@@ -105,6 +105,19 @@
 
     load_rows.start()
     load_cols.start()
+
+    @pl.when(tm == 1)
+    def _():
+        greet(0, cell)
+
+        @pl.when(has_left)
+        def _():
+            greet(0, left)
+
+        @pl.when(has_right)
+        def _():
+            greet(0, right)
+
     for load in load_blocks:
         load.start()
     load_growth.start()
@@ -117,15 +130,6 @@
     @pl.when(tm == 1)
     def _():
         load_last.start()
-        greet(0, cell)
-
-        @pl.when(has_left)
-        def _():
-            greet(0, left)
-
-        @pl.when(has_right)
-        def _():
-            greet(0, right)
 
         def greet_all(step, carry):
             greet(1, lax.rem(cell + step, cells))
@@ -148,7 +152,7 @@
     def block_range(r):
         return pl.ds(r * side, side)
 
-    def column_sums(beside=None):
+    def column_sums():
         total = None
         for step in range(steps):
             places = [step * GROUP + i for i in range(GROUP)]
@@ -159,8 +163,6 @@
                 product = product + jnp.where(index[2, step] > 0, total, 0.0)
             total = product
             partial[step] = total
-            if beside is not None:
-                beside(step)
 
     def column(w):
         return jnp.where(index[4, w] > 0, partial[index[3, w]], 0.0)
@@ -208,7 +210,6 @@
         for load in load_blocks:
             load.wait()
         column_sums()
-        outer_columns()
         load_passed.wait()
         labels_right = remote(labels.at[0], labels.at[0], 7, 1, right)
         labels_left = remote(labels.at[0], labels.at[2], 8, 1, left)
@@ -220,13 +221,21 @@
 
         @pl.when(has_right)
         def _():
+            labels_right.start()
+
+        @pl.when(has_left)
+        def _():
+            labels_left.start()
+
+        outer_columns()
+
+        @pl.when(has_right)
+        def _():
             edge_right.start()
-            labels_right.start()
 
         @pl.when(has_left)
         def _():
             edge_left.start()
-            labels_left.start()
 
         own_columns()
         own_here.start()
@@ -279,6 +288,7 @@
         totals = [row_totals(r) for r in range(dev_blocks)]
         scaled[dev_blocks] = jnp.zeros((height, side), BF16)
         load_growth.wait()
+        per_growth[...] = 1.0 / growth[...]
 
         @pl.when(has_left)
         def _():
@@ -337,29 +347,28 @@
         whole_back = remote(whole, whole, 6, 0, cell)
         whole_back.start()
         mean = jnp.sum(row_sum, axis=1, keepdims=True) * (1.0 / dev_cells)
-        unit = jnp.broadcast_to(jnp.where(mean > 0.0, mean, 1.0), (height, side))
+        unit = jnp.where(mean > 0.0, mean, 1.0)
+        per_unit = 1.0 / unit
         weighted = jnp.zeros((height, side), F32)
         for r in range(dev_blocks):
-            value = (whole[r] / unit / growth[:, block_range(r)]).astype(BF16)
+            value = (whole[r] * per_unit * per_growth[:, block_range(r)]).astype(BF16)
             scaled[r] = value
             weighted = weighted + value.astype(F32) * totals[r]
         remote(first_total, first_total, 11, 0, cell).wait_recv()
-        message[...] = jnp.concatenate([jnp.sum(weighted.T, axis=0, keepdims=True), unit.T[0:1], first_total[...], first_total[...]], axis=0)
+        message[:, 0:height] = jnp.sum(weighted.T, axis=0, keepdims=True)
+        message[:, height : 2 * height] = jnp.broadcast_to(unit, (height, side)).T[0:1]
+        message[:, 2 * height : 3 * height] = first_total[...]
         pl.semaphore_wait(barrier, cells - 1)
 
         def tell(step):
             pltpu.make_async_remote_copy(
                 src_ref=message, dst_ref=messages.at[cell], send_sem=all_send_sem, recv_sem=all_recv_sem,
-                device_id=(1, lax.rem(cell + step, cells)), device_id_type=MESH,
+                device_id=(1, step + lax.div(step + cells - cell, cells)), device_id_type=MESH,
             ).start()
 
-        share = -(-(cells - 1) // steps)
-
-        def tell_some(step):
-            for number in range(1 + step * share, min(1 + (step + 1) * share, cells)):
-                tell(number)
-
-        column_sums(tell_some)
+        for step in range(cells - 1):
+            tell(step)
+        column_sums()
         outer_columns()
         far_left = remote(edges.at[0], far_sum.at[1], 9, 1, left)
         far_right = remote(edges.at[1], far_sum.at[0], 10, 1, right)
@@ -379,14 +388,13 @@
         )
         heard.wait()
         messages[cell] = message[...]
-        first_factor[...] = all_cells / jnp.sum(messages[:, 2, :], axis=0, keepdims=True)
+        first_factor[...] = all_cells / jnp.sum(messages[:, :, 2 * height : 3 * height], axis=0)
         factor_here = remote(first_factor, first_factor, 12, 0, cell)
         factor_here.start()
-        sums, units = messages[:, 0, :], messages[:, 1, :]
-        largest = jnp.max(units, axis=0, keepdims=True)
-        total = jnp.sum(sums * (units / largest), axis=0, keepdims=True)
-        sources = (left, cell, right)
-        factors = [all_cells * (messages[i][1:2] / largest) / total for i in sources]
+        sums, units = messages[:, :, 0:height], messages[:, :, height : 2 * height]
+        per_largest = 1.0 / jnp.max(units, axis=0)
+        common = all_cells / jnp.sum(sums * (units * per_largest), axis=0)
+        factors = [messages[i][:, height : 2 * height] * per_largest * common for i in (left, cell, right)]
         square = jnp.concatenate(factors + [jnp.zeros((height - 3, height), F32)], axis=0).T
         factors = [square[:, i : i + 1] for i in range(3)]
 
@@ -415,6 +423,14 @@
         fate_here.wait_send()
         whole_back.wait_send()
         factor_here.wait_send()
+
+
+def hand_over(mass, fate, mass_out, fate_out, sems):
+    copies = [pltpu.make_async_copy(mass, mass_out, sems.at[0]), pltpu.make_async_copy(fate, fate_out, sems.at[1])]
+    for copy in copies:
+        copy.start()
+    for copy in copies:
+        copy.wait()
 
 
 def on_device(block_rows, block_cols, block_values, growth, first_labels, last_labels):
@@ -428,7 +444,7 @@
     steps = (slots + (GROUP - 1) * columns) // GROUP
     out = jax.ShapeDtypeStruct((1, height, dev_cells), BF16)
     copies = 13
-    return pl.pallas_call(
+    mass, fate = pl.pallas_call(
         kernel,
         out_shape=(out, out),
         in_specs=[pl.BlockSpec(memory_space=pl.ANY)] * 6,
@@ -437,6 +453,7 @@
             pltpu.VMEM((1, slots), jnp.int32),
             pltpu.VMEM((1, slots), jnp.int32),
             pltpu.VMEM((slots, side, side), BF16),
+            pltpu.VMEM((1, dev_cells), F32),
             pltpu.VMEM((1, dev_cells), F32),
             pltpu.VMEM((3, panels, dev_cells), jnp.int32),
             pltpu.VMEM((8, 128), jnp.int32),
@@ -452,8 +469,8 @@
             pltpu.VMEM((dev_blocks, height, side), F32),
             pltpu.VMEM((1, height), F32),
             pltpu.VMEM((1, height), F32),
-            pltpu.VMEM((4, height), F32),
-            pltpu.VMEM((cells, 4, height), F32),
+            pltpu.VMEM((1, 3 * height), F32),
+            pltpu.VMEM((cells, 1, 3 * height), F32),
             pltpu.SemaphoreType.DMA((5,)),
             pltpu.SemaphoreType.DMA((4,)),
             pltpu.SemaphoreType.DMA,
@@ -464,6 +481,13 @@
         ],
         compiler_params=pltpu.CompilerParams(collective_id=0, has_side_effects=True, vmem_limit_bytes=40 * 1024 * 1024),
     )(*[pltpu.with_memory_space_constraint(x, pltpu.HBM) for x in (block_rows, block_cols, block_values, growth, first_labels, last_labels)])
+    return pl.pallas_call(
+        hand_over,
+        out_shape=(out, out),
+        in_specs=[pl.BlockSpec(memory_space=pl.ANY)] * 2,
+        out_specs=(pl.BlockSpec(memory_space=pl.ANY), pl.BlockSpec(memory_space=pl.ANY)),
+        scratch_shapes=[pltpu.SemaphoreType.DMA((2,))],
+    )(pltpu.with_memory_space_constraint(mass, pltpu.VMEM), pltpu.with_memory_space_constraint(fate, pltpu.VMEM))
 
 
 def solution(mesh):

time: 24.8 us -> 22.6 us (0.911)
  local copies, waits for them, and re-layouts: 1.31 us -> 0 us
  Pallas kernels: 22.7 us -> 21.9 us
    pallas_call x1, Pallas kernels: 22.7 us -> 21.1 us  [on_device(): pl.pallas_call(kernel, out_shape=(out, out), in_specs=[pl.BlockSpec(memor...]
    unnamed x2 -> x0, local copies, waits for them, and re-layouts: 1.31 us -> none
    pallas_call x0 -> x1, Pallas kernels: none -> 0.72 us  [on_device(): pl.pallas_call(hand_over, out_shape=(out, out), in_specs=[pl.BlockSpec(me...]
where the time goes in v3:
time: 22.6 us; the launch traced here: 22.5 us
  Pallas kernels  21.9 us (97%)
  between operations  0.64 us (3%)
    pallas_call x1, Pallas kernels, on_device(): pl.pallas_call(kernel, out_shape=(out, out), in_specs=[pl.BlockSpec(memor...  21.1 us
    pallas_call x1, Pallas kernels, on_device(): pl.pallas_call(hand_over, out_shape=(out, out), in_specs=[pl.BlockSpec(me...  0.72 us

profile of v3, /device:TPU:1, one launch (start us, length us, event | category | flops | bytes accessed | tf_op | source)
XLA Modules:
  0.0 22.5 jit_solution(8374262641465677480)
XLA Ops:
  0.6 21.1 %shard_map.77 = (bf16[1,128,512]{2,1,0:T(8,128)(2,1)S(1)}, bf16[1,128,512]{2,1,0:T(8,128)(2,1)S(1)}) custom-call(s32[1,64]{1,0:T(1,128)} %rows_hbm.1, s32[1,64]{1,0:T(1,128)} %cols_hbm.1, bf16[1,64,128,128]{3,2,1,0:T(8,128)(2,1)} %blocks_hbm.1, f32[1,512]{1,0:T(1,128)} %growth_hbm.1, s32[8,512]{1,0:T(8,128)} %first_hbm.1, s32[8,512]{1,0:T(8,128)} %last_hbm.1), custom_call_target="tpu_custom_call" | custom-call | tf_op jit(solution)/shard_map/pallas_call | solution.py:447
  21.8 0.7 %shard_map.78 = (bf16[1,128,512]{2,1,0:T(8,128)(2,1)}, bf16[1,128,512]{2,1,0:T(8,128)(2,1)}) custom-call(bf16[1,128,512]{2,1,0:T(8,128)(2,1)S(1)} %get-tuple-element.4.mass, bf16[1,128,512]{2,1,0:T(8,128)(2,1)S(1)} %get-tuple-element.5.fate), custom_call_target="tpu_custom_call" | custom-call | tf_op jit(solution)/shard_map/pallas_call | solution.py:484

commit v4 on v3

--- a/solution.py
+++ b/solution.py
@@ -9,7 +9,8 @@
 
 CELL_TYPES = 16
 BAND_REACH = 4
-GROUP = 4
+GROUP = 2
+JOIN = 8
 MESH = pl.DeviceIdType.MESH
 F32 = jnp.float32
 BF16 = jnp.bfloat16
@@ -178,8 +179,8 @@
 
     def fate_block(r):
         total = None
-        for k in range(0, per_row, GROUP):
-            places = [r * per_row + k + i for i in range(GROUP)]
+        for k in range(0, per_row, JOIN):
+            places = [r * per_row + k + i for i in range(JOIN)]
             taken = jnp.concatenate([window[index[6, p]] for p in places], axis=1)
             stored = jnp.concatenate([blocks[index[5, p]] for p in places], axis=1)
             product = lax.dot_general(taken, stored, (((1,), (1,)), ((), ())), preferred_element_type=F32)
@@ -189,10 +190,10 @@
         return grouped.reshape(height, side).astype(BF16)
 
     def row_totals(r):
-        ones = jnp.ones((8, GROUP * side), BF16)
+        ones = jnp.ones((8, JOIN * side), BF16)
         total = None
-        for k in range(0, per_row, GROUP):
-            places = [r * per_row + k + i for i in range(GROUP)]
+        for k in range(0, per_row, JOIN):
+            places = [r * per_row + k + i for i in range(JOIN)]
             stored = jnp.concatenate([blocks[index[5, p]] for p in places], axis=1)
             product = lax.dot_general(ones, stored, (((1,), (1,)), ((), ())), preferred_element_type=F32)
             total = product if total is None else total + product
@@ -311,15 +312,6 @@
         fate_here = remote(fates, window.at[pl.ds(reach, dev_blocks)], 4, 0, cell)
         fate_left = remote(fates, window.at[pl.ds(reach + dev_blocks, reach)], 5, 0, left)
 
-        @pl.when(has_right)
-        def _():
-            fate_right.start()
-
-        @pl.when(has_left)
-        def _():
-            fate_left.start()
-
-        fate_here.start()
 
         @pl.when(has_right)
         def _():
@@ -345,7 +337,6 @@
             whole[r] = value
             row_sum = row_sum + value
         whole_back = remote(whole, whole, 6, 0, cell)
-        whole_back.start()
         mean = jnp.sum(row_sum, axis=1, keepdims=True) * (1.0 / dev_cells)
         unit = jnp.where(mean > 0.0, mean, 1.0)
         per_unit = 1.0 / unit
@@ -368,6 +359,16 @@
 
         for step in range(cells - 1):
             tell(step)
+        @pl.when(has_right)
+        def _():
+            fate_right.start()
+
+        @pl.when(has_left)
+        def _():
+            fate_left.start()
+
+        fate_here.start()
+        whole_back.start()
         column_sums()
         outer_columns()
         far_left = remote(edges.at[0], far_sum.at[1], 9, 1, left)

time: 22.6 us -> 21.9 us (0.969)
  Pallas kernels: 21.9 us -> 21.1 us
    pallas_call x1, Pallas kernels: 21.1 us -> 20.4 us  [on_device(): pl.pallas_call(kernel, out_shape=(out, out), in_specs=[pl.BlockSpec(memor...]
where the time goes in v4:
time: 21.9 us; the launch traced here: 21.8 us
  Pallas kernels  21.1 us (96%)
  between operations  0.64 us (3%)
    pallas_call x1, Pallas kernels, on_device(): pl.pallas_call(kernel, out_shape=(out, out), in_specs=[pl.BlockSpec(memor...  20.4 us
    pallas_call x1, Pallas kernels, on_device(): pl.pallas_call(hand_over, out_shape=(out, out), in_specs=[pl.BlockSpec(me...  0.72 us

profile of v4, /device:TPU:1, one launch (start us, length us, event | category | flops | bytes accessed | tf_op | source)
XLA Modules:
  0.0 21.8 jit_solution(323187827799797668)
XLA Ops:
  0.6 20.4 %shard_map.77 = (bf16[1,128,512]{2,1,0:T(8,128)(2,1)S(1)}, bf16[1,128,512]{2,1,0:T(8,128)(2,1)S(1)}) custom-call(s32[1,64]{1,0:T(1,128)} %rows_hbm.1, s32[1,64]{1,0:T(1,128)} %cols_hbm.1, bf16[1,64,128,128]{3,2,1,0:T(8,128)(2,1)} %blocks_hbm.1, f32[1,512]{1,0:T(1,128)} %growth_hbm.1, s32[8,512]{1,0:T(8,128)} %first_hbm.1, s32[8,512]{1,0:T(8,128)} %last_hbm.1), custom_call_target="tpu_custom_call" | custom-call | tf_op jit(solution)/shard_map/pallas_call | solution.py:448
  21.1 0.7 %shard_map.78 = (bf16[1,128,512]{2,1,0:T(8,128)(2,1)}, bf16[1,128,512]{2,1,0:T(8,128)(2,1)}) custom-call(bf16[1,128,512]{2,1,0:T(8,128)(2,1)S(1)} %get-tuple-element.4.mass, bf16[1,128,512]{2,1,0:T(8,128)(2,1)S(1)} %get-tuple-element.5.fate), custom_call_target="tpu_custom_call" | custom-call | tf_op jit(solution)/shard_map/pallas_call | solution.py:485

commit v5 on v3

--- a/solution.py
+++ b/solution.py
@@ -9,7 +9,8 @@
 
 CELL_TYPES = 16
 BAND_REACH = 4
-GROUP = 4
+GROUP = 2
+JOIN = 8
 MESH = pl.DeviceIdType.MESH
 F32 = jnp.float32
 BF16 = jnp.bfloat16
@@ -70,7 +71,7 @@
 def kernel(
     rows_hbm, cols_hbm, blocks_hbm, growth_hbm, first_hbm, last_hbm, mass_out, fate_out,
     rows, cols, blocks, growth, per_growth, labels, table, index, scaled, window, partial, edges, own_sum, fates,
-    near_sum, far_sum, whole, first_total, first_factor, message, messages,
+    near_sum, far_sum, spare, whole, weights, weights_left, far_unit, first_total, first_factor, message, messages,
     load_sem, block_sem, index_sem, send_sem, recv_sem, all_send_sem, all_recv_sem,
 ):
     tm, cell = lax.axis_index("tm"), lax.axis_index("cell")
@@ -178,8 +179,8 @@
 
     def fate_block(r):
         total = None
-        for k in range(0, per_row, GROUP):
-            places = [r * per_row + k + i for i in range(GROUP)]
+        for k in range(0, per_row, JOIN):
+            places = [r * per_row + k + i for i in range(JOIN)]
             taken = jnp.concatenate([window[index[6, p]] for p in places], axis=1)
             stored = jnp.concatenate([blocks[index[5, p]] for p in places], axis=1)
             product = lax.dot_general(taken, stored, (((1,), (1,)), ((), ())), preferred_element_type=F32)
@@ -189,10 +190,10 @@
         return grouped.reshape(height, side).astype(BF16)
 
     def row_totals(r):
-        ones = jnp.ones((8, GROUP * side), BF16)
+        ones = jnp.ones((8, JOIN * side), BF16)
         total = None
-        for k in range(0, per_row, GROUP):
-            places = [r * per_row + k + i for i in range(GROUP)]
+        for k in range(0, per_row, JOIN):
+            places = [r * per_row + k + i for i in range(JOIN)]
             stored = jnp.concatenate([blocks[index[5, p]] for p in places], axis=1)
             product = lax.dot_general(ones, stored, (((1,), (1,)), ((), ())), preferred_element_type=F32)
             total = product if total is None else total + product
@@ -216,6 +217,7 @@
         edge_left = remote(edges.at[0], near_sum.at[1], 0, 1, left)
         edge_right = remote(edges.at[1], near_sum.at[0], 1, 1, right)
         own_here = remote(own_sum, whole, 2, 1, cell)
+        spare_here = remote(edges.at[0], spare, 13, 1, cell)
         total_here = remote(first_total, first_total, 11, 1, cell)
         pl.semaphore_wait(barrier, 2 + lax.div(cell + cells - 1, cells) - lax.div(cell + 1, cells))
 
@@ -236,6 +238,7 @@
         @pl.when(has_left)
         def _():
             edge_left.start()
+            spare_here.start()
 
         own_columns()
         own_here.start()
@@ -268,6 +271,7 @@
         def _():
             edge_left.wait_send()
             labels_left.wait_send()
+            spare_here.wait_send()
 
         own_here.wait_send()
         total_here.wait_send()
@@ -289,96 +293,123 @@
         scaled[dev_blocks] = jnp.zeros((height, side), BF16)
         load_growth.wait()
         per_growth[...] = 1.0 / growth[...]
-
-        @pl.when(has_left)
-        def _():
-            remote(labels.at[0], labels.at[0], 7, 0, left).wait_recv()
-            for r in range(reach):
-                window[r] = one_hot(labels[0, :, block_range(dev_blocks - reach + r)]).astype(BF16)
-
-        @pl.when(has_right)
-        def _():
-            remote(labels.at[0], labels.at[2], 8, 0, right).wait_recv()
-            for r in range(reach):
-                window[reach + dev_blocks + r] = one_hot(labels[2, :, block_range(r)]).astype(BF16)
-
-        for r in range(dev_blocks):
-            value = fate_block(r)
-            fates[r] = value
-            fate_out[0, :, block_range(r)] = value
+        for r in range(dev_blocks):
+            weights[:, block_range(r)] = totals[r] * per_growth[:, block_range(r)]
+        pl.semaphore_wait(barrier, cells - 1)
+        weights_right = remote(weights, weights_left, 14, 1, right)
+
+        @pl.when(has_right)
+        def _():
+            weights_right.start()
+
         remote(own_sum, whole, 2, 0, cell).wait_recv()
         fate_right = remote(fates, window.at[pl.ds(0, reach)], 3, 0, right)
         fate_here = remote(fates, window.at[pl.ds(reach, dev_blocks)], 4, 0, cell)
         fate_left = remote(fates, window.at[pl.ds(reach + dev_blocks, reach)], 5, 0, left)
 
-        @pl.when(has_right)
-        def _():
-            fate_right.start()
-
-        @pl.when(has_left)
-        def _():
-            fate_left.start()
-
-        fate_here.start()
-
-        @pl.when(has_right)
-        def _():
-            remote(edges.at[0], near_sum.at[1], 0, 0, right).wait_recv()
-
-        @pl.when(has_left)
-        def _():
+
+        @pl.when(has_left)
+        def _():
+            remote(edges.at[0], spare, 13, 0, cell).wait_recv()
+            remote(weights, weights_left, 14, 1, left).wait_recv()
             remote(edges.at[1], near_sum.at[0], 1, 0, left).wait_recv()
+
+        @pl.when(jnp.logical_not(has_left))
+        def _():
+            near_sum[0] = jnp.zeros(near_sum.shape[1:], BF16)
+            far_sum[0] = jnp.zeros(far_sum.shape[1:], BF16)
+            spare[...] = jnp.zeros(spare.shape, BF16)
+            weights_left[...] = jnp.zeros(weights_left.shape, F32)
+            far_unit[0] = jnp.zeros((1, height), F32)
 
         @pl.when(jnp.logical_not(has_right))
         def _():
             near_sum[1] = jnp.zeros(near_sum.shape[1:], BF16)
             far_sum[1] = jnp.zeros(far_sum.shape[1:], BF16)
-
-        @pl.when(jnp.logical_not(has_left))
-        def _():
-            near_sum[0] = jnp.zeros(near_sum.shape[1:], BF16)
-            far_sum[0] = jnp.zeros(far_sum.shape[1:], BF16)
+            far_unit[2] = jnp.zeros((1, height), F32)
 
         row_sum = jnp.zeros((height, side), F32)
-        for r in range(dev_blocks):
-            value = whole[r] + near_sum[0, r].astype(F32) + near_sum[1, r].astype(F32)
+        weighted = jnp.zeros((height, side), F32)
+        for r in range(dev_blocks):
+            value = whole[r] + near_sum[0, r].astype(F32)
+            whole[r] = value
+            row_sum = row_sum + value + spare[r].astype(F32)
+        mean = jnp.sum(row_sum, axis=1, keepdims=True) * (1.0 / dev_cells)
+        per_unit = 1.0 / jnp.where(mean > 0.0, mean, 1.0)
+        for r in range(dev_blocks):
+            weighted = weighted + whole[r] * per_unit * weights[:, block_range(r)]
+            weighted = weighted + spare[r].astype(F32) * per_unit * weights_left[:, block_range(r)]
+        remote(first_total, first_total, 11, 0, cell).wait_recv()
+        message[:, 0:height] = jnp.sum(weighted.T, axis=0, keepdims=True)
+        message[:, height : 2 * height] = jnp.broadcast_to(mean, (height, side)).T[0:1]
+        message[:, 2 * height : 3 * height] = first_total[...]
+
+        def tell(step):
+            pltpu.make_async_remote_copy(
+                src_ref=message, dst_ref=messages.at[cell], send_sem=all_send_sem, recv_sem=all_recv_sem,
+                device_id=(1, step + lax.div(step + cells - cell, cells)), device_id_type=MESH,
+            ).start()
+
+        for step in range(cells - 1):
+            tell(step)
+
+        @pl.when(has_left)
+        def _():
+            remote(labels.at[0], labels.at[0], 7, 0, left).wait_recv()
+            for r in range(reach):
+                window[r] = one_hot(labels[0, :, block_range(dev_blocks - reach + r)]).astype(BF16)
+
+        @pl.when(has_right)
+        def _():
+            remote(labels.at[0], labels.at[2], 8, 0, right).wait_recv()
+            for r in range(reach):
+                window[reach + dev_blocks + r] = one_hot(labels[2, :, block_range(r)]).astype(BF16)
+
+        for r in range(dev_blocks):
+            value = fate_block(r)
+            fates[r] = value
+            fate_out[0, :, block_range(r)] = value
+        @pl.when(has_right)
+        def _():
+            fate_right.start()
+
+        @pl.when(has_left)
+        def _():
+            fate_left.start()
+
+        fate_here.start()
+
+        @pl.when(has_right)
+        def _():
+            remote(edges.at[0], near_sum.at[1], 0, 0, right).wait_recv()
+
+        row_sum = jnp.zeros((height, side), F32)
+        for r in range(dev_blocks):
+            value = whole[r] + near_sum[1, r].astype(F32)
             whole[r] = value
             row_sum = row_sum + value
         whole_back = remote(whole, whole, 6, 0, cell)
         whole_back.start()
         mean = jnp.sum(row_sum, axis=1, keepdims=True) * (1.0 / dev_cells)
-        unit = jnp.where(mean > 0.0, mean, 1.0)
-        per_unit = 1.0 / unit
-        weighted = jnp.zeros((height, side), F32)
-        for r in range(dev_blocks):
-            value = (whole[r] * per_unit * per_growth[:, block_range(r)]).astype(BF16)
-            scaled[r] = value
-            weighted = weighted + value.astype(F32) * totals[r]
-        remote(first_total, first_total, 11, 0, cell).wait_recv()
-        message[:, 0:height] = jnp.sum(weighted.T, axis=0, keepdims=True)
-        message[:, height : 2 * height] = jnp.broadcast_to(unit, (height, side)).T[0:1]
-        message[:, 2 * height : 3 * height] = first_total[...]
-        pl.semaphore_wait(barrier, cells - 1)
-
-        def tell(step):
-            pltpu.make_async_remote_copy(
-                src_ref=message, dst_ref=messages.at[cell], send_sem=all_send_sem, recv_sem=all_recv_sem,
-                device_id=(1, step + lax.div(step + cells - cell, cells)), device_id_type=MESH,
-            ).start()
-
-        for step in range(cells - 1):
-            tell(step)
+        per_unit = 1.0 / jnp.where(mean > 0.0, mean, 1.0)
+        for r in range(dev_blocks):
+            scaled[r] = (whole[r] * per_unit * per_growth[:, block_range(r)]).astype(BF16)
+        far_unit[1] = jnp.broadcast_to(mean, (height, side)).T[0:1]
         column_sums()
         outer_columns()
         far_left = remote(edges.at[0], far_sum.at[1], 9, 1, left)
         far_right = remote(edges.at[1], far_sum.at[0], 10, 1, right)
-
-        @pl.when(has_right)
-        def _():
+        unit_left = remote(far_unit.at[1], far_unit.at[2], 15, 1, left)
+        unit_right = remote(far_unit.at[1], far_unit.at[0], 16, 1, right)
+
+        @pl.when(has_right)
+        def _():
+            unit_right.start()
             far_right.start()
 
         @pl.when(has_left)
         def _():
+            unit_left.start()
             far_left.start()
 
         own_columns()
@@ -394,18 +425,19 @@
         sums, units = messages[:, :, 0:height], messages[:, :, height : 2 * height]
         per_largest = 1.0 / jnp.max(units, axis=0)
         common = all_cells / jnp.sum(sums * (units * per_largest), axis=0)
-        factors = [messages[i][:, height : 2 * height] * per_largest * common for i in (left, cell, right)]
+        @pl.when(has_left)
+        def _():
+            remote(far_unit.at[1], far_unit.at[0], 16, 1, left).wait_recv()
+            remote(edges.at[1], far_sum.at[0], 10, 1, left).wait_recv()
+
+        @pl.when(has_right)
+        def _():
+            remote(far_unit.at[1], far_unit.at[2], 15, 1, right).wait_recv()
+            remote(edges.at[0], far_sum.at[1], 9, 1, right).wait_recv()
+
+        factors = [far_unit[i] * per_largest * common for i in range(3)]
         square = jnp.concatenate(factors + [jnp.zeros((height - 3, height), F32)], axis=0).T
         factors = [square[:, i : i + 1] for i in range(3)]
-
-        @pl.when(has_left)
-        def _():
-            remote(edges.at[1], far_sum.at[0], 10, 1, left).wait_recv()
-
-        @pl.when(has_right)
-        def _():
-            remote(edges.at[0], far_sum.at[1], 9, 1, right).wait_recv()
-
         for r in range(dev_blocks):
             value = own_sum[r] * factors[1] + far_sum[0, r].astype(F32) * factors[0] + far_sum[1, r].astype(F32) * factors[2]
             mass_out[0, :, block_range(r)] = value.astype(BF16)
@@ -414,11 +446,14 @@
         def _():
             fate_right.wait_send()
             far_right.wait_send()
+            unit_right.wait_send()
+            weights_right.wait_send()
 
         @pl.when(has_left)
         def _():
             fate_left.wait_send()
             far_left.wait_send()
+            unit_left.wait_send()
 
         fate_here.wait_send()
         whole_back.wait_send()
@@ -443,7 +478,7 @@
     columns = dev_blocks + 2 * BAND_REACH
     steps = (slots + (GROUP - 1) * columns) // GROUP
     out = jax.ShapeDtypeStruct((1, height, dev_cells), BF16)
-    copies = 13
+    copies = 17
     mass, fate = pl.pallas_call(
         kernel,
         out_shape=(out, out),
@@ -466,7 +501,11 @@
             pltpu.VMEM((dev_blocks, height, side), BF16),
             pltpu.VMEM((2, BAND_REACH, height, side), BF16),
             pltpu.VMEM((2, BAND_REACH, height, side), BF16),
+            pltpu.VMEM((BAND_REACH, height, side), BF16),
             pltpu.VMEM((dev_blocks, height, side), F32),
+            pltpu.VMEM((1, dev_cells), F32),
+            pltpu.VMEM((1, dev_cells), F32),
+            pltpu.VMEM((3, 1, height), F32),
             pltpu.VMEM((1, height), F32),
             pltpu.VMEM((1, height), F32),
             pltpu.VMEM((1, 3 * height), F32),

time: 22.6 us -> 19.9 us (0.88)
  Pallas kernels: 21.9 us -> 19.1 us
    pallas_call x1, Pallas kernels: 21.1 us -> 18.4 us  [on_device(): pl.pallas_call(kernel, out_shape=(out, out), in_specs=[pl.BlockSpec(memor...]
where the time goes in v5:
time: 19.9 us; the launch traced here: 19.8 us
  Pallas kernels  19.1 us (96%)
  between operations  0.64 us (3%)
    pallas_call x1, Pallas kernels, on_device(): pl.pallas_call(kernel, out_shape=(out, out), in_specs=[pl.BlockSpec(memor...  18.4 us
    pallas_call x1, Pallas kernels, on_device(): pl.pallas_call(hand_over, out_shape=(out, out), in_specs=[pl.BlockSpec(me...  0.72 us

profile of v5, /device:TPU:1, one launch (start us, length us, event | category | flops | bytes accessed | tf_op | source)
XLA Modules:
  0.0 19.8 jit_solution(13550548679111375787)
XLA Ops:
  0.6 18.4 %shard_map.77 = (bf16[1,128,512]{2,1,0:T(8,128)(2,1)S(1)}, bf16[1,128,512]{2,1,0:T(8,128)(2,1)S(1)}) custom-call(s32[1,64]{1,0:T(1,128)} %rows_hbm.1, s32[1,64]{1,0:T(1,128)} %cols_hbm.1, bf16[1,64,128,128]{3,2,1,0:T(8,128)(2,1)} %blocks_hbm.1, f32[1,512]{1,0:T(1,128)} %growth_hbm.1, s32[8,512]{1,0:T(8,128)} %first_hbm.1, s32[8,512]{1,0:T(8,128)} %last_hbm.1), custom_call_target="tpu_custom_call" | custom-call | tf_op jit(solution)/shard_map/pallas_call | solution.py:482
  19.0 0.7 %shard_map.78 = (bf16[1,128,512]{2,1,0:T(8,128)(2,1)}, bf16[1,128,512]{2,1,0:T(8,128)(2,1)}) custom-call(bf16[1,128,512]{2,1,0:T(8,128)(2,1)S(1)} %get-tuple-element.4.mass, bf16[1,128,512]{2,1,0:T(8,128)(2,1)S(1)} %get-tuple-element.5.fate), custom_call_target="tpu_custom_call" | custom-call | tf_op jit(solution)/shard_map/pallas_call | solution.py:523

commit v6 on v5

--- a/solution.py
+++ b/solution.py
@@ -71,7 +71,7 @@
 def kernel(
     rows_hbm, cols_hbm, blocks_hbm, growth_hbm, first_hbm, last_hbm, mass_out, fate_out,
     rows, cols, blocks, growth, per_growth, labels, table, index, scaled, window, partial, edges, own_sum, fates,
-    near_sum, far_sum, spare, whole, weights, weights_left, far_unit, first_total, first_factor, message, messages,
+    near_sum, far_sum, spare, whole, part, entire, weights, weights_left, far_unit, first_total, first_factor, message, messages,
     load_sem, block_sem, index_sem, send_sem, recv_sem, all_send_sem, all_recv_sem,
 ):
     tm, cell = lax.axis_index("tm"), lax.axis_index("cell")
@@ -134,9 +134,12 @@
 
         def greet_all(step, carry):
             greet(1, lax.rem(cell + step, cells))
+            greet(1, lax.rem(cell + cells - step, cells))
             return carry
 
-        lax.fori_loop(1, cells, greet_all, 0)
+        lax.fori_loop(1, (cells + 1) // 2, greet_all, 0)
+        if cells % 2 == 0:
+            greet(1, lax.rem(cell + cells // 2, cells))
 
     load_rows.wait()
     load_cols.wait()
@@ -295,24 +298,12 @@
         per_growth[...] = 1.0 / growth[...]
         for r in range(dev_blocks):
             weights[:, block_range(r)] = totals[r] * per_growth[:, block_range(r)]
-        pl.semaphore_wait(barrier, cells - 1)
         weights_right = remote(weights, weights_left, 14, 1, right)
 
-        @pl.when(has_right)
-        def _():
-            weights_right.start()
-
-        remote(own_sum, whole, 2, 0, cell).wait_recv()
         fate_right = remote(fates, window.at[pl.ds(0, reach)], 3, 0, right)
         fate_here = remote(fates, window.at[pl.ds(reach, dev_blocks)], 4, 0, cell)
         fate_left = remote(fates, window.at[pl.ds(reach + dev_blocks, reach)], 5, 0, left)
 
-
-        @pl.when(has_left)
-        def _():
-            remote(edges.at[0], spare, 13, 0, cell).wait_recv()
-            remote(weights, weights_left, 14, 1, left).wait_recv()
-            remote(edges.at[1], near_sum.at[0], 1, 0, left).wait_recv()
 
         @pl.when(jnp.logical_not(has_left))
         def _():
@@ -328,72 +319,106 @@
             far_sum[1] = jnp.zeros(far_sum.shape[1:], BF16)
             far_unit[2] = jnp.zeros((1, height), F32)
 
+        def take_left():
+            remote(own_sum, whole, 2, 0, cell).wait_recv()
+
+            @pl.when(has_left)
+            def _():
+                remote(edges.at[1], near_sum.at[0], 1, 0, left).wait_recv()
+
+        def give_weights():
+            @pl.when(has_right)
+            def _():
+                weights_right.start()
+
+        def report():
+            @pl.when(has_left)
+            def _():
+                remote(edges.at[0], spare, 13, 0, cell).wait_recv()
+                remote(weights, weights_left, 14, 1, left).wait_recv()
+
+            row_sum = jnp.zeros((height, side), F32)
+            weighted = jnp.zeros((height, side), F32)
+            for r in range(dev_blocks):
+                value = whole[r] + near_sum[0, r].astype(F32)
+                part[r] = value
+                row_sum = row_sum + value + spare[r].astype(F32)
+            mean = jnp.sum(row_sum, axis=1, keepdims=True) * (1.0 / dev_cells)
+            per_unit = 1.0 / jnp.where(mean > 0.0, mean, 1.0)
+            for r in range(dev_blocks):
+                weighted = weighted + part[r] * per_unit * weights[:, block_range(r)]
+                weighted = weighted + spare[r].astype(F32) * per_unit * weights_left[:, block_range(r)]
+            remote(first_total, first_total, 11, 0, cell).wait_recv()
+            message[:, 0:height] = jnp.sum(weighted.T, axis=0, keepdims=True)
+            message[:, height : 2 * height] = jnp.broadcast_to(mean, (height, side)).T[0:1]
+            message[:, 2 * height : 3 * height] = first_total[...]
+
+            def tell(step):
+                pltpu.make_async_remote_copy(
+                    src_ref=message, dst_ref=messages.at[cell], send_sem=all_send_sem, recv_sem=all_recv_sem,
+                    device_id=(1, step + lax.div(step + cells - cell, cells)), device_id_type=MESH,
+                ).start()
+
+            for step in range(cells - 1):
+                tell(step)
+
+        def go_back():
+            @pl.when(has_left)
+            def _():
+                remote(labels.at[0], labels.at[0], 7, 0, left).wait_recv()
+                for r in range(reach):
+                    window[r] = one_hot(labels[0, :, block_range(dev_blocks - reach + r)]).astype(BF16)
+
+            @pl.when(has_right)
+            def _():
+                remote(labels.at[0], labels.at[2], 8, 0, right).wait_recv()
+                for r in range(reach):
+                    window[reach + dev_blocks + r] = one_hot(labels[2, :, block_range(r)]).astype(BF16)
+
+            for r in range(dev_blocks):
+                value = fate_block(r)
+                fates[r] = value
+                fate_out[0, :, block_range(r)] = value
+            @pl.when(has_right)
+            def _():
+                fate_right.start()
+
+            @pl.when(has_left)
+            def _():
+                fate_left.start()
+
+            fate_here.start()
+
+        early = (cell < 13) | (cell == 16)
+
+        @pl.when(jnp.logical_not(early))
+        def _():
+            pl.semaphore_wait(barrier, cells - 1)
+            give_weights()
+            take_left()
+            report()
+            go_back()
+
+        @pl.when(has_right)
+        def _():
+            remote(edges.at[0], near_sum.at[1], 0, 0, right).wait_recv()
+
+        @pl.when(early)
+        def _():
+            give_weights()
+            take_left()
+
         row_sum = jnp.zeros((height, side), F32)
-        weighted = jnp.zeros((height, side), F32)
-        for r in range(dev_blocks):
-            value = whole[r] + near_sum[0, r].astype(F32)
-            whole[r] = value
-            row_sum = row_sum + value + spare[r].astype(F32)
-        mean = jnp.sum(row_sum, axis=1, keepdims=True) * (1.0 / dev_cells)
-        per_unit = 1.0 / jnp.where(mean > 0.0, mean, 1.0)
-        for r in range(dev_blocks):
-            weighted = weighted + whole[r] * per_unit * weights[:, block_range(r)]
-            weighted = weighted + spare[r].astype(F32) * per_unit * weights_left[:, block_range(r)]
-        remote(first_total, first_total, 11, 0, cell).wait_recv()
-        message[:, 0:height] = jnp.sum(weighted.T, axis=0, keepdims=True)
-        message[:, height : 2 * height] = jnp.broadcast_to(mean, (height, side)).T[0:1]
-        message[:, 2 * height : 3 * height] = first_total[...]
-
-        def tell(step):
-            pltpu.make_async_remote_copy(
-                src_ref=message, dst_ref=messages.at[cell], send_sem=all_send_sem, recv_sem=all_recv_sem,
-                device_id=(1, step + lax.div(step + cells - cell, cells)), device_id_type=MESH,
-            ).start()
-
-        for step in range(cells - 1):
-            tell(step)
-
-        @pl.when(has_left)
-        def _():
-            remote(labels.at[0], labels.at[0], 7, 0, left).wait_recv()
-            for r in range(reach):
-                window[r] = one_hot(labels[0, :, block_range(dev_blocks - reach + r)]).astype(BF16)
-
-        @pl.when(has_right)
-        def _():
-            remote(labels.at[0], labels.at[2], 8, 0, right).wait_recv()
-            for r in range(reach):
-                window[reach + dev_blocks + r] = one_hot(labels[2, :, block_range(r)]).astype(BF16)
-
-        for r in range(dev_blocks):
-            value = fate_block(r)
-            fates[r] = value
-            fate_out[0, :, block_range(r)] = value
-        @pl.when(has_right)
-        def _():
-            fate_right.start()
-
-        @pl.when(has_left)
-        def _():
-            fate_left.start()
-
-        fate_here.start()
-
-        @pl.when(has_right)
-        def _():
-            remote(edges.at[0], near_sum.at[1], 0, 0, right).wait_recv()
-
-        row_sum = jnp.zeros((height, side), F32)
-        for r in range(dev_blocks):
-            value = whole[r] + near_sum[1, r].astype(F32)
-            whole[r] = value
+        for r in range(dev_blocks):
+            value = whole[r] + near_sum[0, r].astype(F32) + near_sum[1, r].astype(F32)
+            entire[r] = value
             row_sum = row_sum + value
-        whole_back = remote(whole, whole, 6, 0, cell)
+        whole_back = remote(entire, whole, 6, 0, cell)
         whole_back.start()
         mean = jnp.sum(row_sum, axis=1, keepdims=True) * (1.0 / dev_cells)
         per_unit = 1.0 / jnp.where(mean > 0.0, mean, 1.0)
         for r in range(dev_blocks):
-            scaled[r] = (whole[r] * per_unit * per_growth[:, block_range(r)]).astype(BF16)
+            scaled[r] = (entire[r] * per_unit * per_growth[:, block_range(r)]).astype(BF16)
         far_unit[1] = jnp.broadcast_to(mean, (height, side)).T[0:1]
         column_sums()
         outer_columns()
@@ -413,6 +438,13 @@
             far_left.start()
 
         own_columns()
+
+        @pl.when(early)
+        def _():
+            pl.semaphore_wait(barrier, cells - 1)
+            report()
+            go_back()
+
         heard = pltpu.make_async_remote_copy(
             src_ref=messages.at[pl.ds(0, cells - 1)], dst_ref=messages.at[pl.ds(0, cells - 1)],
             send_sem=all_send_sem, recv_sem=all_recv_sem, device_id=(1, lax.rem(cell + 1, cells)), device_id_type=MESH,
@@ -503,6 +535,8 @@
             pltpu.VMEM((2, BAND_REACH, height, side), BF16),
             pltpu.VMEM((BAND_REACH, height, side), BF16),
             pltpu.VMEM((dev_blocks, height, side), F32),
+            pltpu.VMEM((dev_blocks, height, side), F32),
+            pltpu.VMEM((dev_blocks, height, side), F32),
             pltpu.VMEM((1, dev_cells), F32),
             pltpu.VMEM((1, dev_cells), F32),
             pltpu.VMEM((3, 1, height), F32),

time: 19.9 us -> 19.9 us (level)
  no operation moved by 1% of the time
where the time goes in v6:
time: 19.9 us; the launch traced here: 19.8 us
  Pallas kernels  19.1 us (96%)
  between operations  0.64 us (3%)
    pallas_call x1, Pallas kernels, on_device(): pl.pallas_call(kernel, out_shape=(out, out), in_specs=[pl.BlockSpec(memor...  18.4 us
    pallas_call x1, Pallas kernels, on_device(): pl.pallas_call(hand_over, out_shape=(out, out), in_specs=[pl.BlockSpec(me...  0.72 us

profile of v6, /device:TPU:1, one launch (start us, length us, event | category | flops | bytes accessed | tf_op | source)
XLA Modules:
  0.0 19.8 jit_solution(2641397639944001263)
XLA Ops:
  0.6 18.4 %shard_map.77 = (bf16[1,128,512]{2,1,0:T(8,128)(2,1)S(1)}, bf16[1,128,512]{2,1,0:T(8,128)(2,1)S(1)}) custom-call(s32[1,64]{1,0:T(1,128)} %rows_hbm.1, s32[1,64]{1,0:T(1,128)} %cols_hbm.1, bf16[1,64,128,128]{3,2,1,0:T(8,128)(2,1)} %blocks_hbm.1, f32[1,512]{1,0:T(1,128)} %growth_hbm.1, s32[8,512]{1,0:T(8,128)} %first_hbm.1, s32[8,512]{1,0:T(8,128)} %last_hbm.1), custom_call_target="tpu_custom_call" | custom-call | tf_op jit(solution)/shard_map/pallas_call | solution.py:514
  19.0 0.7 %shard_map.78 = (bf16[1,128,512]{2,1,0:T(8,128)(2,1)}, bf16[1,128,512]{2,1,0:T(8,128)(2,1)}) custom-call(bf16[1,128,512]{2,1,0:T(8,128)(2,1)S(1)} %get-tuple-element.4.mass, bf16[1,128,512]{2,1,0:T(8,128)(2,1)S(1)} %get-tuple-element.5.fate), custom_call_target="tpu_custom_call" | custom-call | tf_op jit(solution)/shard_map/pallas_call | solution.py:557

commit v7 on v6

--- a/solution.py
+++ b/solution.py
@@ -241,10 +241,14 @@
         @pl.when(has_left)
         def _():
             edge_left.start()
-            spare_here.start()
 
         own_columns()
         own_here.start()
+
+        @pl.when(has_left)
+        def _():
+            spare_here.start()
+
         row_sum = own_sum[0]
         for w in range(1, dev_blocks):
             row_sum = row_sum + own_sum[w]

time: 19.9 us -> 19.9 us (level)
  no operation moved by 1% of the time
where the time goes in v7:
time: 19.9 us; the launch traced here: 19.8 us
  Pallas kernels  19.1 us (96%)
  between operations  0.64 us (3%)
    pallas_call x1, Pallas kernels, on_device(): pl.pallas_call(kernel, out_shape=(out, out), in_specs=[pl.BlockSpec(memor...  18.4 us
    pallas_call x1, Pallas kernels, on_device(): pl.pallas_call(hand_over, out_shape=(out, out), in_specs=[pl.BlockSpec(me...  0.72 us

profile of v7, /device:TPU:1, one launch (start us, length us, event | category | flops | bytes accessed | tf_op | source)
XLA Modules:
  0.0 19.8 jit_solution(15370325668936663837)
XLA Ops:
  0.6 18.4 %shard_map.77 = (bf16[1,128,512]{2,1,0:T(8,128)(2,1)S(1)}, bf16[1,128,512]{2,1,0:T(8,128)(2,1)S(1)}) custom-call(s32[1,64]{1,0:T(1,128)} %rows_hbm.1, s32[1,64]{1,0:T(1,128)} %cols_hbm.1, bf16[1,64,128,128]{3,2,1,0:T(8,128)(2,1)} %blocks_hbm.1, f32[1,512]{1,0:T(1,128)} %growth_hbm.1, s32[8,512]{1,0:T(8,128)} %first_hbm.1, s32[8,512]{1,0:T(8,128)} %last_hbm.1), custom_call_target="tpu_custom_call" | custom-call | tf_op jit(solution)/shard_map/pallas_call | solution.py:518
  19.0 0.7 %shard_map.78 = (bf16[1,128,512]{2,1,0:T(8,128)(2,1)}, bf16[1,128,512]{2,1,0:T(8,128)(2,1)}) custom-call(bf16[1,128,512]{2,1,0:T(8,128)(2,1)S(1)} %get-tuple-element.4.mass, bf16[1,128,512]{2,1,0:T(8,128)(2,1)S(1)} %get-tuple-element.5.fate), custom_call_target="tpu_custom_call" | custom-call | tf_op jit(solution)/shard_map/pallas_call | solution.py:561
